TPU v7x, 512 devices: a whole 4x8x8 slice. The times are simulated.
512 devices in a mesh: rows: 16 (over z, y_lo), feat: 8 (over x, core), leaf: 4 (over y_hi).
Axes of the slice: x: 4, y: 8 (y_hi: 4, y_lo: 2; y = y_hi * 2 + y_lo), z: 8, core: 2. Of those that a mesh axis runs over, the one named last changes fastest.
Arguments:
- features: float32 [512, 32768], P(None, ('rows', 'feat')), may hold values from -4 to 4
- labels: int32 [32768], P(('rows', 'feat')), may hold values from 0 to 63
- weights: bfloat16 [4, 32768], P('leaf', ('rows', 'feat')), may hold values from 0.0009994507 to 4
- nodes: int32 [4, 32768], P('leaf', ('rows', 'feat')), may hold values from 0 to 1
Outputs:
- split_gain: float32 [4, 2, 512], P('leaf', None, ('rows', 'feat'))
- node_best: float32 [4, 2], P('leaf')
All inputs are finite; a program needn't handle non-finite values.
Results may differ from a plain program's by a relative error of at most 0.0003.
Values may be sent and summed in bfloat16 or wider, within the bound.
A program may use at most 64 MiB of HBM per device.

v0:
```python
import math

import jax
import jax.numpy as jnp
from jax import lax
from jax.sharding import PartitionSpec as P

B = 128
C = 64
NODES = 2


def edge_table(bin_count, dtype):
    positions = jnp.arange(bin_count - 1, dtype=dtype)
    return (positions + 1.0 - bin_count // 2) * (9.0 / bin_count)


def split_scores(cumulative):
    totals = cumulative[..., -1:, :, :]
    right_side = totals - cumulative

    def ratio_sum(values):
        return jnp.sum(values * values, axis=-1) / jnp.maximum(jnp.sum(values, axis=-1), 1.0)

    split_value = ratio_sum(cumulative) + ratio_sum(right_side) - ratio_sum(totals)
    return jnp.max(split_value, axis=-2)


def build_targets(row_labels, row_weights, row_nodes):
    row_total = row_labels.shape[0]
    node_hit = row_nodes.T[:, :, None] == jnp.arange(NODES, dtype=jnp.int32)
    class_hit = (row_labels[:, None] == jnp.arange(C, dtype=jnp.int32)).astype(jnp.bfloat16)
    weighted = jnp.where(node_hit, row_weights.T[:, :, None], jnp.zeros((), jnp.bfloat16))
    target = weighted[:, :, :, None] * class_hit[:, None, None, :]
    return target.reshape(row_total, -1)


def local_histograms(columns, target):
    feature_total, row_total = columns.shape
    bin_count = B
    edge_values = edge_table(bin_count, jnp.float32)
    row_limit = max(1, (1 << 21) // (bin_count * row_total))
    group_size = math.gcd(feature_total, row_limit)

    def per_group(feature_set):
        below_edges = feature_set[:, None, :] <= edge_values[None, :, None]
        all_rows = jnp.ones((group_size, 1, row_total), jnp.bool_)
        below_mask = jnp.concatenate([below_edges, all_rows], axis=1).astype(jnp.bfloat16)
        return jnp.einsum("fbr,rk->fbk", below_mask, target, preferred_element_type=jnp.float32)

    grouped = columns.reshape(feature_total // group_size, group_size, row_total)
    results = lax.map(per_group, grouped)
    return results.reshape(feature_total, bin_count, -1)


def local(features, labels, weights, nodes):
    feature_total = features.shape[0]
    entry_rows = features.shape[1]
    tree_count = weights.shape[0]
    owned = feature_total // (lax.axis_size("rows") * lax.axis_size("feat"))
    shaped = features.reshape(lax.axis_size("rows"), lax.axis_size("feat"), owned, entry_rows)
    arrived = lax.all_to_all(shaped, "feat", split_axis=1, concat_axis=3, tiled=True)
    columns = arrived.reshape(lax.axis_size("rows") * owned, -1)
    row_labels, row_nodes = (
        lax.all_gather(labels, "feat", axis=0, tiled=True),
        lax.all_gather(nodes, "feat", axis=1, tiled=True),
    )
    row_weights = lax.all_gather(weights, "feat", axis=1, tiled=True)
    partial_value = local_histograms(columns, build_targets(row_labels, row_weights, row_nodes))
    summed = lax.psum(partial_value, "rows")
    cumulative = lax.dynamic_slice_in_dim(summed, lax.axis_index("rows") * owned, owned, 0)
    grouped_hist = cumulative.reshape(
        cumulative.shape[0], cumulative.shape[1], tree_count * NODES, C
    )
    scores = split_scores(grouped_hist)
    split_gain = scores.T.reshape(tree_count, NODES, -1)
    node_best = lax.pmax(jnp.max(split_gain, axis=2), ("rows", "feat"))
    return (split_gain, node_best)


def solution(mesh):
    return jax.shard_map(
        local,
        mesh=mesh,
        in_specs=(
            P(None, ("rows", "feat")),
            P(("rows", "feat")),
            P("leaf", ("rows", "feat")),
            P("leaf", ("rows", "feat")),
        ),
        out_specs=(P("leaf", None, ("rows", "feat")), P("leaf", None)),
        check_vma=False,
    )
```

profile of v0, /device:TPU:1, one launch (start us, length us, event | category | flops | bytes accessed | tf_op | source)
XLA Modules:
  0.0 572.6 jit_solution(15278984202766600189)
XLA Ops:
  7.2 1.2 reshape.107
  9.2 10.2 %all-to-all-start = ((f32[16,8,4,256]{3,2,0,1:T(4,128)}), f32[16,8,4,256]{3,2,0,1:T(4,128)S(1)}, u32[]{:S(2)}, u32[]{:S(2)}) async-start(f32[16,8,4,256]{3,2,0,1:T(4,128)} %copy.20), calls=%async_computation | async-start | bytes 1048576 | tf_op jit(solution)/shard_map/all_to_all | solution.py:62
  19.4 13.1 %all_gather.10 = bf16[1,2048]{1,0:T(2,128)(2,1)S(1)} all-gather(bf16[1,256]{1,0:T(2,128)(2,1)} %param.8), channel_id=1, replica_groups=mesh['rows'=16,'feat'=8,'leaf'=4] {'feat'}, dimensions={1}, use_global_device_ids=true | all-gather | bytes 4608 | tf_op jit(solution)/shard_map/all_gather | solution.py:68
  32.6 9.2 %all_gather.9 = s32[1,2048]{1,0:T(1,128)S(1)} all-gather(s32[1,256]{1,0:T(1,128)} %param.9), channel_id=1, replica_groups=mesh['rows'=16,'feat'=8,'leaf'=4] {'feat'}, dimensions={1}, use_global_device_ids=true | all-gather | bytes 9216 | tf_op jit(solution)/shard_map/all_gather | solution.py:66
  41.8 8.9 %all-gather = s32[8,1,256]{2,1,0:T(1,128)S(1)} all-gather(s32[1,1,256]{2,1,0:T(1,128)} %bitcast.45), channel_id=1, replica_groups=mesh['rows'=16,'feat'=8,'leaf'=4] {'feat'}, dimensions={0}, use_global_device_ids=true | all-gather | bytes 9216 | tf_op jit(solution)/shard_map/all_gather | solution.py:65
  51.2 30.6 %while.11 = (s32[]{:T(128)}, f32[8,8,128,128]{2,3,1,0:T(8,128)}, f32[8,8,2048]{2,1,0:T(8,128)S(1)}, bf16[2048,64]{0,1:T(8,128)(2,1)S(1)}, bf16[2048,2]{0,1:T(2,128)(2,1)S(1)}, /*index=5*/s32[]{:T(128)}) while((s32[]{:T(128)}, f32[8,8,128,128]{2,3,1,0:T(8,128)}, f32[8,8,2048]{2,1,0:T(8,128)S(1)}, bf16[2048,64]{0,1:T(8,128)(2,1)S(1)}, ...), condition=%wide.region_1.2_spmd.clone, body=%wide.region_0.1_spmd.clone.sunk | while | flops 539214080 | bytes 6202945 | solution.py:52
  51.2 1.4 broadcast_compare_fusion.2
  52.7 2.3 fusion.21
  55.0 1.4 broadcast_compare_fusion.2
  56.5 2.3 fusion.21
  58.9 1.4 broadcast_compare_fusion.2
  60.3 2.4 fusion.21
  62.7 1.4 broadcast_compare_fusion.2
  64.2 2.3 fusion.21
  66.5 1.4 broadcast_compare_fusion.2
  68.0 2.3 fusion.21
  70.3 1.4 broadcast_compare_fusion.2
  71.8 2.3 fusion.21
  74.2 1.4 broadcast_compare_fusion.2
  75.6 2.3 fusion.21
  78.0 1.4 broadcast_compare_fusion.2
  79.4 2.3 fusion.21
  81.8 203.8 %all-reduce.3.cloned.1.call-done = f32[64,128,128]{1,2,0:T(8,128)} async-done(((f32[64,128,128]{1,2,0:T(8,128)}), f32[64,128,128]{1,2,0:T(8,128)}) %all-reduce.3.cloned.1.call-update) | async-done | bytes 4194320 | tf_op jit(solution)/shard_map/psum | solution.py:70
  288.9 276.9 %pmax.7 = f32[1,2]{1,0:T(1,128)} all-reduce(f32[1,2]{1,0:T(1,128)S(1)} %bitcast.47), channel_id=1, replica_groups=mesh['rows'=16,'feat'=8,'leaf'=4] {'rows','feat'}, use_global_device_ids=true, to_apply=%region_11.12 | all-reduce | flops 2 | bytes 16 | tf_op jit(solution)/shard_map/pmax | solution.py:77
  (40 shorter events, 5.1 us)
Async XLA Ops:
  9.2 41.6 %all-to-all-start = ((f32[16,8,4,256]{3,2,0,1:T(4,128)}), f32[16,8,4,256]{3,2,0,1:T(4,128)S(1)}, u32[]{:S(2)}, u32[]{:S(2)}) async-start(f32[16,8,4,256]{3,2,0,1:T(4,128)} %copy.20), calls=%async_computation | async-start | bytes 1048576 | tf_op jit(solution)/shard_map/all_to_all | solution.py:62
  19.4 266.2 %all-reduce.3.cloned.1.call-start = ((), (), s32[]{:S(2)}) async-start(), calls=%async_computation.1 | async-start | bytes 8388608 | tf_op jit(solution)/shard_map/psum | solution.py:70
Sparse Core Ops, SparseCore 0:
  81.9 203.6 all-reduce.2
where the time goes:
time: 574 us; the launch traced here: 573 us
  blocking collectives  308 us (54%)
  waiting for transfers between devices  204 us (36%)
  matrix products  18.7 us (3%)
  between operations  14.1 us (2%)
  other arithmetic  13.4 us (2%)
  starting transfers between devices  10.2 us (2%)
    pmax x1, blocking collectives, local(): node_best = lax.pmax(jnp.max(split_gain, axis=2), ('rows', 'feat'))  277 us
    psum x1, waiting for transfers between devices, local(): summed = lax.psum(partial_value, 'rows')  204 us
    dot_general x8, matrix products, per_group(): jnp.einsum('fbr,rk->fbk', below_mask, target, preferred_element_type=jnp....  18.7 us
    all_gather x1, blocking collectives, local(): row_weights = lax.all_gather(weights, 'feat', axis=1, tiled=True)  13.1 us
  transfers between devices with their start and end apart: 2, of which 1 were waited for; matrix products, arithmetic and copies ran while one was open for 0% of the time, Pallas kernels for 0%

commit v1 on v0

v1 whole, which is shorter than its diff:
```python
import functools

import jax
import jax.numpy as jnp
from jax import lax
from jax.experimental import pallas as pl
from jax.experimental.pallas import tpu as pltpu
from jax.sharding import PartitionSpec as P

B = 128
C = 64
NODES = 2
OWN = 4
Z = 8
Y = 2
X = 4
CORES = 2
ROWS_AX = Z * Y
FEAT_AX = X * CORES
LOCAL = 256
GROUP = 2
f32 = jnp.float32
bf16 = jnp.bfloat16
MESH = pl.DeviceIdType.MESH
NT = (((1,), (1,)), ((), ()))
ORDER = [(0, 0), (0, 1), (1, 0), (7, 0), (1, 1), (7, 1), (2, 0), (6, 0), (2, 1), (6, 1), (3, 0), (5, 0), (3, 1), (5, 1), (4, 0), (4, 1)]


def bin_index(x):
    guess = jnp.clip(jnp.ceil(x * (B / 9.0) + (B // 2 - 1)), 0.0, B - 1.0)
    edge_here = (guess + (1.0 - B // 2)) * (9.0 / B)
    edge_before = (guess - (1.0 * (B // 2))) * (9.0 / B)
    up = jnp.where((edge_here < x) & (guess < B - 1.0), 1.0, 0.0)
    down = jnp.where((edge_before >= x) & (guess > 0.0), 1.0, 0.0)
    return guess + up - down


def row_pack(tile, row):
    return jnp.broadcast_to(tile[row : row + 1, :], (16, 128)).astype(bf16)


def mask_tile(tile, bins):
    one, zero = jnp.ones((), bf16), jnp.zeros((), bf16)
    rows = []
    for i in range(OWN):
        halves = []
        for h in range(2):
            packed = row_pack(tile, h * 4 + i)
            halves.append(jnp.where(packed[None] <= bins, one, zero).reshape(B, 128))
        rows.append(jnp.concatenate(halves, axis=1))
    return jnp.concatenate(rows, axis=0)


def target_tile(tile, classes):
    zero = jnp.zeros((), bf16)
    parts = [[], []]
    for h in range(2):
        hit = row_pack(tile, h * 4)[None] == classes
        for n in range(NODES):
            weight = jnp.broadcast_to(row_pack(tile, h * 4 + 1 + n)[None], hit.shape)
            parts[n].append(jnp.where(hit, weight, zero).reshape(C, 128))
    return jnp.concatenate([jnp.concatenate(p, axis=1) for p in parts], axis=0)


def ratio(values):
    return jnp.sum(values * values, axis=0, keepdims=True) / jnp.maximum(jnp.sum(values, axis=0, keepdims=True), 1.0)


def kernel(
    feat_hbm, lab_ref, wei_ref, node_ref, gain_ref, best_ref,
    feat_v, send, own_codes, zbuf, zcode, rbuf, rcode, acc, m1s, m1, m2s, m2,
    in_sem, s1_send, s1_recv, c1_send, c1_recv, s2_send, s2_recv, c2_send, c2_recv, m1_send, m1_recv, m2_send, m2_recv,
):
    my_rows, my_feat = lax.axis_index("rows"), lax.axis_index("feat")
    z, y = lax.div(my_rows, Y), lax.rem(my_rows, Y)
    loads = []
    for q in range(4):
        part = pl.ds(q * 128, 128)
        loads.append(pltpu.make_async_copy(feat_hbm.at[part], feat_v.at[part], in_sem.at[q]))
        loads[-1].start()

    def rows_peer(dz, dy):
        return lax.rem(z + dz, Z) * Y + lax.rem(y + dy, Y)

    def feat_peer(d):
        return lax.rem(my_feat + d, FEAT_AX)

    barrier = pltpu.get_barrier_semaphore()
    for dz, dy in ORDER[1:]:
        pl.semaphore_signal(barrier, inc=1, device_id={"rows": rows_peer(dz, dy)}, device_id_type=MESH)
    for d in range(1, FEAT_AX):
        pl.semaphore_signal(barrier, inc=1, device_id={"feat": feat_peer(d)}, device_id_type=MESH)

    label = lab_ref[...].astype(f32)
    weight = wei_ref[...].astype(f32)
    node = node_ref[...]
    w0 = jnp.where(node == 0, weight, 0.0)
    w1 = jnp.where(node == 1, weight, 0.0)
    pad = jnp.zeros_like(w0)
    lines = []
    for h in range(2):
        cut = slice(h * 128, (h + 1) * 128)
        lines += [label[:, cut], w0[:, cut], w1[:, cut], pad[:, cut]]
    own_codes[...] = jnp.concatenate(lines, axis=0).astype(bf16)

    sub = lax.broadcasted_iota(jnp.int32, (4, 8, 128), 1)
    for q in range(4):
        loads[q].wait()

        def place(r, carry):
            values = bin_index(feat_v[pl.ds(pl.multiple_of(r * 32, 32), 32), :])
            a = values[:, :128].reshape(4, 8, 128)
            b = values[:, 128:].reshape(4, 8, 128)
            first = jnp.where(sub < 4, a, pltpu.roll(b, 4, 1))
            second = jnp.where(sub < 4, pltpu.roll(a, 4, 1), b)
            both = jnp.stack([first, second], axis=1).reshape(8, 8, 128)
            send[r] = both.astype(bf16)
            return carry

        lax.fori_loop(q * 4, q * 4 + 4, place, 0)

    pl.semaphore_wait(barrier, ROWS_AX - 1 + FEAT_AX - 1)

    first_copies = {}
    for s in range(1, ROWS_AX):
        peer = rows_peer(*ORDER[s])
        first_copies[s] = (
            pltpu.make_async_remote_copy(
                src_ref=send.at[peer], dst_ref=zbuf.at[s], send_sem=s1_send.at[s], recv_sem=s1_recv.at[s],
                device_id={"rows": peer}, device_id_type=MESH),
            pltpu.make_async_remote_copy(
                src_ref=own_codes, dst_ref=zcode.at[s], send_sem=c1_send.at[s], recv_sem=c1_recv.at[s],
                device_id={"rows": peer}, device_id_type=MESH),
        )
        for copy in first_copies[s]:
            copy.start()

    def forward(s):
        if s > 0:
            for copy in first_copies[s]:
                copy.wait_recv()
        for d in range(1, FEAT_AX):
            peer = feat_peer(d)
            source = zbuf.at[s, peer] if s > 0 else send.at[my_rows, peer]
            pltpu.make_async_remote_copy(
                src_ref=source, dst_ref=rbuf.at[s, d], send_sem=s2_send.at[s], recv_sem=s2_recv.at[s],
                device_id={"feat": peer}, device_id_type=MESH).start()
            pltpu.make_async_remote_copy(
                src_ref=zcode.at[s] if s > 0 else own_codes, dst_ref=rcode.at[s, d], send_sem=c2_send.at[s], recv_sem=c2_recv.at[s],
                device_id={"feat": peer}, device_id_type=MESH).start()

    def all_of(buffer, s, sem):
        part = buffer.at[s, pl.ds(1, FEAT_AX - 1)]
        return pltpu.make_async_copy(part, part, sem.at[s])

    bins = (lax.broadcasted_iota(jnp.int32, (8, 16, 128), 0) * 16 + lax.broadcasted_iota(jnp.int32, (8, 16, 128), 1)).astype(f32).astype(bf16)
    classes = bins[: C // 16]
    acc[...] = jnp.zeros_like(acc)

    def use(slots):
        masks, targets = [], []
        for s in slots:
            all_of(rbuf, s, s2_recv).wait()
            all_of(rcode, s, c2_recv).wait()
        for s in slots:
            mine = zbuf[s, my_feat] if s > 0 else send[my_rows, my_feat]
            codes = zcode[s] if s > 0 else own_codes[...]
            masks.append(mask_tile(mine.astype(f32), bins))
            targets.append(target_tile(codes.astype(f32), classes))
            for d in range(1, FEAT_AX):
                masks.append(mask_tile(rbuf[s, d].astype(f32), bins))
                targets.append(target_tile(rcode[s, d].astype(f32), classes))
        acc[...] += lax.dot_general(jnp.concatenate(masks, axis=1), jnp.concatenate(targets, axis=1), NT, preferred_element_type=f32)

    groups = [list(range(g, g + GROUP)) for g in range(0, ROWS_AX, GROUP)]
    for g, slots in enumerate(groups):
        for s in slots:
            forward(s)
        if g >= 1:
            use(groups[g - 1])
    use(groups[-1])

    row_at = lax.broadcasted_iota(jnp.int32, (8, 128), 0)
    lane_at = lax.broadcasted_iota(jnp.int32, (8, 128), 1)
    gains = jnp.zeros((8, 128), f32)
    best = jnp.zeros((8, 128), f32)
    for n in range(NODES):
        node_top = None
        for i in range(OWN):
            left = acc[i * B : (i + 1) * B, :].T[n * C : (n + 1) * C, :]
            total = left[:, B - 1 : B]
            right = total - left
            gain = ratio(left) + ratio(right) - ratio(total)
            top = jnp.max(gain, axis=1, keepdims=True)
            gains = jnp.where((row_at == n) & (lane_at == i), top, gains)
            node_top = top if node_top is None else jnp.maximum(node_top, top)
        best = jnp.where(row_at == n, node_top, best)
    gain_ref[0] = gains[:NODES, :OWN]

    m1s[...] = best
    copies = []
    for d in range(1, FEAT_AX):
        copies.append(pltpu.make_async_remote_copy(
            src_ref=m1s, dst_ref=m1.at[d], send_sem=m1_send.at[d], recv_sem=m1_recv.at[d],
            device_id={"feat": feat_peer(d)}, device_id_type=MESH))
        copies[-1].start()
    for d, copy in enumerate(copies, 1):
        copy.wait_recv()
        best = jnp.maximum(best, m1[d])
    m2s[...] = best
    for s in range(1, ROWS_AX):
        copies.append(pltpu.make_async_remote_copy(
            src_ref=m2s, dst_ref=m2.at[s], send_sem=m2_send.at[s], recv_sem=m2_recv.at[s],
            device_id={"rows": rows_peer(*ORDER[s])}, device_id_type=MESH))
        copies[-1].start()
    for s, copy in enumerate(copies[FEAT_AX - 1 :], 1):
        copy.wait_recv()
        best = jnp.maximum(best, m2[s])
    row2 = lax.broadcasted_iota(jnp.int32, (1, NODES), 1)
    best_ref[...] = jnp.where(row2 == 0, best[0:1, :NODES], best[1:2, :NODES])

    for copy in copies:
        copy.wait_send()
    for s in range(ROWS_AX):
        if s > 0:
            for copy in first_copies[s]:
                copy.wait_send()
        all_of(rbuf, s, s2_send).wait()
        all_of(rcode, s, c2_send).wait()


def local(features, labels, weights, nodes):
    dma = pltpu.SemaphoreType.DMA
    return pl.pallas_call(
        kernel,
        out_shape=(
            jax.ShapeDtypeStruct((1, NODES, OWN), f32),
            jax.ShapeDtypeStruct((1, NODES), f32),
        ),
        in_specs=[pl.BlockSpec(memory_space=pl.ANY)] + [pl.BlockSpec(memory_space=pltpu.VMEM)] * 3,
        out_specs=(pl.BlockSpec(memory_space=pltpu.VMEM),) * 2,
        scratch_shapes=[
            pltpu.VMEM((512, LOCAL), f32),
            pltpu.VMEM((ROWS_AX, FEAT_AX, 8, 128), bf16),
            pltpu.VMEM((8, 128), bf16),
            pltpu.VMEM((ROWS_AX, FEAT_AX, 8, 128), bf16),
            pltpu.VMEM((ROWS_AX, 8, 128), bf16),
            pltpu.VMEM((ROWS_AX, FEAT_AX, 8, 128), bf16),
            pltpu.VMEM((ROWS_AX, FEAT_AX, 8, 128), bf16),
            pltpu.VMEM((OWN * B, NODES * C), f32),
            pltpu.VMEM((8, 128), f32),
            pltpu.VMEM((FEAT_AX, 8, 128), f32),
            pltpu.VMEM((8, 128), f32),
            pltpu.VMEM((ROWS_AX, 8, 128), f32),
            dma((4,)),
            dma((ROWS_AX,)), dma((ROWS_AX,)), dma((ROWS_AX,)), dma((ROWS_AX,)),
            dma((ROWS_AX,)), dma((ROWS_AX,)), dma((ROWS_AX,)), dma((ROWS_AX,)),
            dma((FEAT_AX,)), dma((FEAT_AX,)), dma((ROWS_AX,)), dma((ROWS_AX,)),
        ],
        compiler_params=pltpu.CompilerParams(collective_id=0, has_side_effects=True, vmem_limit_bytes=48 * 1024 * 1024),
        name="split_scores",
    )(features, labels.reshape(1, -1), weights, nodes)


def solution(mesh):
    return jax.shard_map(
        local,
        mesh=mesh,
        in_specs=(
            P(None, ("rows", "feat")),
            P(("rows", "feat")),
            P("leaf", ("rows", "feat")),
            P("leaf", ("rows", "feat")),
        ),
        out_specs=(P("leaf", None, ("rows", "feat")), P("leaf", None)),
        check_vma=False,
    )
```

time: 574 us -> 60.3 us (0.11)
  blocking collectives: 308 us -> 0 us
  waiting for transfers between devices: 204 us -> 0 us
  Pallas kernels: 0 us -> 55.3 us
  matrix products: 18.7 us -> 0 us
  between operations: 14.1 us -> 0.65 us
  other arithmetic: 13.4 us -> 0 us
  starting transfers between devices: 10.2 us -> 0 us
    pmax x1 -> x0, blocking collectives: 277 us -> none  [local(): node_best = lax.pmax(jnp.max(split_gain, axis=2), ('rows', 'feat'))]
    psum x1 -> x0, waiting for transfers between devices: 204 us -> none  [local(): summed = lax.psum(partial_value, 'rows')]
    pallas_call x0 -> x1, Pallas kernels: none -> 55.3 us  [local(): pl.pallas_call(kernel, out_shape=(jax.ShapeDtypeStruct((1, NODES, OWN), f...]
    all_gather x3 -> x0, blocking collectives: 31.3 us -> none  [the longest x1 13.1 us: local(): row_weights = lax.all_gather(weights, 'feat', axis=1, tiled=True)]
    dot_general x8 -> x0, matrix products: 18.7 us -> none  [per_group(): jnp.einsum('fbr,rk->fbk', below_mask, target, preferred_element_type=jnp....]
    le x8 -> x0, other arithmetic: 11.3 us -> none  [per_group(): below_edges = feature_set[:, None, :] <= edge_values[None, :, None]]
    all_to_all x1 -> x0, starting transfers between devices: 10.2 us -> none  [local(): lax.all_to_all(shaped, 'feat', split_axis=1, concat_axis=3, tiled=True)]
  transfers between devices with their start and end apart: 2 -> 0, of which waited for: 1 -> 0; matrix products, arithmetic and copies ran while one was open for 0% -> 0% of each run, Pallas kernels for 0% -> 0%
where the time goes in v1:
time: 60.3 us; the launch traced here: 60.1 us
  Pallas kernels  55.3 us (92%)
  local copies, waits for them, and re-layouts  4.14 us (7%)
  between operations  0.65 us (1%)
    pallas_call x1, Pallas kernels, local(): pl.pallas_call(kernel, out_shape=(jax.ShapeDtypeStruct((1, NODES, OWN), f...  55.3 us
    unnamed x10, local copies, waits for them, and re-layouts  4.14 us

profile of v1, /device:TPU:1, one launch (start us, length us, event | category | flops | bytes accessed | tf_op | source)
XLA Modules:
  0.0 60.1 jit_solution(11449241188524958733)
XLA Ops:
  0.6 0.0 copy-start.1
  0.6 0.7 %copy-done.1 = s32[256]{0:T(256)S(1)} copy-done((s32[256]{0:T(256)S(1)}, s32[256]{0:T(256)}, u32[]{:S(2)}) %copy-start.1) | copy-done | bytes 1048
  1.3 0.0 copy-start
  1.3 1.0 %copy-done = f32[512,256]{1,0:T(8,128)S(1)} copy-done((f32[512,256]{1,0:T(8,128)S(1)}, f32[512,256]{1,0:T(8,128)}, u32[]{:S(2)}) %copy-start) | copy-done | bytes 524312
  2.4 0.0 copy-start.2
  2.4 0.7 %copy-done.2 = bf16[1,256]{1,0:T(2,128)(2,1)S(1)} copy-done((bf16[1,256]{1,0:T(2,128)(2,1)S(1)}, bf16[1,256]{1,0:T(2,128)(2,1)}, u32[]{:S(2)}) %copy-start.2) | copy-done | bytes 536
  3.0 0.0 copy-start.3
  3.0 0.7 %copy-done.3 = s32[1,256]{1,0:T(1,128)S(1)} copy-done((s32[1,256]{1,0:T(1,128)S(1)}, s32[1,256]{1,0:T(1,128)}, u32[]{:S(2)}) %copy-start.3) | copy-done | bytes 1048
  3.7 55.3 %split_scores.1 = (f32[1,2,4]{2,1,0:T(2,128)S(1)}, f32[1,2]{1,0:T(1,128)S(1)}) custom-call(f32[512,256]{1,0:T(8,128)S(1)} %copy-done, s32[1,256]{1,0:T(1,128)S(1)} %bitcast.1, bf16[1,256]{1,0:T(2,128)(2,1)S(1)} %copy-done.2, s32[1,256]{1,0:T(1,128)S(1)} %copy-done.3), custom_call_target="tpu_custom_call" | custom-call | tf_op jit(solution)/shard_map/split_scores/pallas_call | solution.py:234
  59.0 0.6 copy.8
  59.6 0.5 copy.9
Async XLA Ops:
  0.6 0.7 %copy-start.1 = (s32[256]{0:T(256)S(1)}, s32[256]{0:T(256)}, u32[]{:S(2)}) copy-start(s32[256]{0:T(256)} %param.5) | copy-start | bytes 3076
  1.3 1.0 %copy-start = (f32[512,256]{1,0:T(8,128)S(1)}, f32[512,256]{1,0:T(8,128)}, u32[]{:S(2)}) copy-start(f32[512,256]{1,0:T(8,128)} %feat_hbm.1) | copy-start | bytes 1572868
  2.4 0.7 %copy-start.2 = (bf16[1,256]{1,0:T(2,128)(2,1)S(1)}, bf16[1,256]{1,0:T(2,128)(2,1)}, u32[]{:S(2)}) copy-start(bf16[1,256]{1,0:T(2,128)(2,1)} %wei_ref.1) | copy-start | bytes 1540
  3.0 0.7 %copy-start.3 = (s32[1,256]{1,0:T(1,128)S(1)}, s32[1,256]{1,0:T(1,128)}, u32[]{:S(2)}) copy-start(s32[1,256]{1,0:T(1,128)} %node_ref.1) | copy-start | bytes 3076

commit v2 on v1

v2 whole, which is shorter than its diff:
```python
import jax
import jax.numpy as jnp
from jax import lax
from jax.experimental import pallas as pl
from jax.experimental.pallas import tpu as pltpu
from jax.sharding import PartitionSpec as P

B = 128
C = 64
NODES = 2
OWN = 4
Z = 8
Y = 2
X = 4
CORES = 2
ROWS_AX = Z * Y
FEAT_AX = X * CORES
LOCAL = 256
GROUP = 2
AHEAD = 2
f32 = jnp.float32
bf16 = jnp.bfloat16
MESH = pl.DeviceIdType.MESH
NT = (((1,), (1,)), ((), ()))
ORDER = [(0, 0), (0, 1), (1, 0), (7, 0), (1, 1), (7, 1), (2, 0), (6, 0), (2, 1), (6, 1), (3, 0), (5, 0), (3, 1), (5, 1), (4, 0), (4, 1)]


def bin_index(x):
    guess = jnp.clip(jnp.ceil(x * (B / 9.0) + (B // 2 - 1)), 0.0, B - 1.0)
    edge_here = (guess + (1.0 - B // 2)) * (9.0 / B)
    edge_before = (guess - (1.0 * (B // 2))) * (9.0 / B)
    up = jnp.where((edge_here < x) & (guess < B - 1.0), 1.0, 0.0)
    down = jnp.where((edge_before >= x) & (guess > 0.0), 1.0, 0.0)
    return guess + up - down


def row_pack(tile, row):
    return jnp.broadcast_to(tile[row : row + 1, :], (16, 128)).astype(bf16)


def mask_tile(tile, bins):
    one, zero = jnp.ones((), bf16), jnp.zeros((), bf16)
    rows = []
    for i in range(OWN):
        halves = []
        for h in range(2):
            packed = row_pack(tile, h * 4 + i)
            halves.append(jnp.where(packed[None] <= bins, one, zero).reshape(B, 128))
        rows.append(jnp.concatenate(halves, axis=1))
    return jnp.concatenate(rows, axis=0)


def target_tile(tile, classes):
    zero = jnp.zeros((), bf16)
    parts = [[], []]
    for h in range(2):
        hit = row_pack(tile, h * 4)[None] == classes
        for n in range(NODES):
            weight = jnp.broadcast_to(row_pack(tile, h * 4 + 1 + n)[None], hit.shape)
            parts[n].append(jnp.where(hit, weight, zero).reshape(C, 128))
    return jnp.concatenate([jnp.concatenate(p, axis=1) for p in parts], axis=0)


def ratio(values):
    return jnp.sum(values * values, axis=0, keepdims=True) / jnp.maximum(jnp.sum(values, axis=0, keepdims=True), 1.0)


def kernel(
    feat_hbm, lab_hbm, wei_hbm, node_hbm, out_ref,
    feat_v, lab_v, wei_v, node_v, send, zbuf, rbuf, acc, m1s, m1, m2s, m2,
    in_sem, s1_send, s1_recv, s2_send, s2_recv, m1_send, m1_recv, m2_send, m2_recv,
):
    my_rows, my_feat = lax.axis_index("rows"), lax.axis_index("feat")
    z, y = lax.div(my_rows, Y), lax.rem(my_rows, Y)

    def rows_peer(dz, dy):
        return lax.rem(z + dz, Z) * Y + lax.rem(y + dy, Y)

    def feat_peer(d):
        return lax.rem(my_feat + d, FEAT_AX)

    barrier = pltpu.get_barrier_semaphore()
    for dz, dy in reversed(ORDER[1:]):
        pl.semaphore_signal(barrier, inc=1, device_id={"rows": rows_peer(dz, dy)}, device_id_type=MESH)
    for d in range(1, FEAT_AX):
        pl.semaphore_signal(barrier, inc=1, device_id={"feat": feat_peer(d)}, device_id_type=MESH)

    loads = [
        pltpu.make_async_copy(feat_hbm, feat_v, in_sem.at[0]),
        pltpu.make_async_copy(lab_hbm, lab_v, in_sem.at[1]),
        pltpu.make_async_copy(wei_hbm, wei_v, in_sem.at[2]),
        pltpu.make_async_copy(node_hbm, node_v, in_sem.at[3]),
    ]
    for load in loads:
        load.start()
    for load in loads:
        load.wait()

    label = lab_v[...].astype(f32)
    weight = wei_v[...].astype(f32)
    node = node_v[...]
    w0 = jnp.where(node == 0, weight, 0.0)
    w1 = jnp.where(node == 1, weight, 0.0)
    pad = jnp.zeros_like(w0)
    lines = []
    for h in range(2):
        cut = slice(h * 128, (h + 1) * 128)
        lines += [label[:, cut], w0[:, cut], w1[:, cut], pad[:, cut]]
    codes = jnp.concatenate(lines, axis=0).astype(bf16)
    sub = lax.broadcasted_iota(jnp.int32, (4, 8, 128), 1)

    def binned(r):
        values = bin_index(feat_v[pl.ds(pl.multiple_of(r * 32, 32), 32), :])
        a = values[:, :128].reshape(4, 8, 128)
        b = values[:, 128:].reshape(4, 8, 128)
        first = jnp.where(sub < 4, a, pltpu.roll(b, 4, 1))
        second = jnp.where(sub < 4, pltpu.roll(a, 4, 1), b)
        return jnp.stack([first, second], axis=1).reshape(8, 8, 128).astype(bf16)

    def place(r, carry):
        send[r, :FEAT_AX] = binned(r)
        send[r, FEAT_AX] = codes
        return carry

    lax.fori_loop(0, ROWS_AX, place, 0)
    zbuf[0, :FEAT_AX] = binned(my_rows)
    zbuf[0, FEAT_AX] = codes
    acc[...] = jnp.zeros_like(acc)

    pl.semaphore_wait(barrier, ROWS_AX - 1 + FEAT_AX - 1)

    for s in range(1, ROWS_AX):
        peer = rows_peer(*ORDER[s])
        pltpu.make_async_remote_copy(
            src_ref=send.at[peer], dst_ref=zbuf.at[s], send_sem=s1_send, recv_sem=s1_recv.at[s],
            device_id={"rows": peer}, device_id_type=MESH).start()

    def forward(s, wait=True):
        if wait:
            pltpu.make_async_copy(zbuf.at[s], zbuf.at[s], s1_recv.at[s]).wait()
        for d in range(1, FEAT_AX):
            peer = feat_peer(d)
            for part, block in ((0, peer), (1, FEAT_AX)):
                pltpu.make_async_remote_copy(
                    src_ref=zbuf.at[s, block], dst_ref=rbuf.at[s, d, part], send_sem=s2_send, recv_sem=s2_recv.at[s],
                    device_id={"feat": peer}, device_id_type=MESH).start()

    bins = (lax.broadcasted_iota(jnp.int32, (8, 16, 128), 0) * 16 + lax.broadcasted_iota(jnp.int32, (8, 16, 128), 1)).astype(f32).astype(bf16)
    classes = bins[: C // 16]

    def use(g):
        masks, targets = [], []
        for u in range(GROUP):
            part = rbuf.at[g * GROUP + u, pl.ds(1, FEAT_AX - 1)]
            pltpu.make_async_copy(part, part, s2_recv.at[g * GROUP + u]).wait()
        for u in range(GROUP):
            s = g * GROUP + u
            masks.append(mask_tile(zbuf[s, my_feat].astype(f32), bins))
            targets.append(target_tile(zbuf[s, FEAT_AX].astype(f32), classes))
            for d in range(1, FEAT_AX):
                masks.append(mask_tile(rbuf[s, d, 0].astype(f32), bins))
                targets.append(target_tile(rbuf[s, d, 1].astype(f32), classes))
        acc[...] += lax.dot_general(jnp.concatenate(masks, axis=1), jnp.concatenate(targets, axis=1), NT, preferred_element_type=f32)

    forward(0, wait=False)
    for s in range(1, AHEAD * GROUP):
        forward(s)

    def step(g, carry):
        for u in range(GROUP):
            forward((g + AHEAD) * GROUP + u)
        use(g)
        return carry

    def tail(g, carry):
        use(g)
        return carry

    steps = ROWS_AX // GROUP
    lax.fori_loop(0, steps - AHEAD, step, 0)
    lax.fori_loop(steps - AHEAD, steps, tail, 0)

    row_at = lax.broadcasted_iota(jnp.int32, (8, 128), 0)
    lane_at = lax.broadcasted_iota(jnp.int32, (8, 128), 1)
    gains = jnp.zeros((8, 128), f32)
    best = jnp.zeros((8, 128), f32)
    for n in range(NODES):
        node_top = None
        for i in range(OWN):
            left = acc[i * B : (i + 1) * B, :].T[n * C : (n + 1) * C, :]
            total = left[:, B - 1 : B]
            right = total - left
            gain = ratio(left) + ratio(right) - ratio(total)
            top = jnp.max(gain, axis=1, keepdims=True)
            gains = jnp.where((row_at == n) & (lane_at == i), top, gains)
            node_top = top if node_top is None else jnp.maximum(node_top, top)
        best = jnp.where(row_at == n, node_top, best)

    m1s[...] = best
    for d in range(1, FEAT_AX):
        pltpu.make_async_remote_copy(
            src_ref=m1s, dst_ref=m1.at[d], send_sem=m1_send, recv_sem=m1_recv,
            device_id={"feat": feat_peer(d)}, device_id_type=MESH).start()
    m1_all, m2_all = m1.at[pl.ds(1, FEAT_AX - 1)], m2.at[pl.ds(1, ROWS_AX - 1)]
    pltpu.make_async_copy(m1_all, m1_all, m1_recv).wait()
    best = jnp.maximum(best, jnp.max(m1[1:], axis=0))
    m2s[...] = best
    for s in range(1, ROWS_AX):
        pltpu.make_async_remote_copy(
            src_ref=m2s, dst_ref=m2.at[s], send_sem=m2_send, recv_sem=m2_recv,
            device_id={"rows": rows_peer(*ORDER[s])}, device_id_type=MESH).start()
    z_all, r_all = zbuf.at[pl.ds(1, ROWS_AX - 1)], rbuf.at[:, pl.ds(1, FEAT_AX - 1)]
    pltpu.make_async_copy(z_all, z_all, s1_send).wait()
    pltpu.make_async_copy(r_all, r_all, s2_send).wait()
    pltpu.make_async_copy(m1_all, m1_all, m1_send).wait()
    pltpu.make_async_copy(m2_all, m2_all, m2_send).wait()
    pltpu.make_async_copy(m2_all, m2_all, m2_recv).wait()
    best = jnp.maximum(best, jnp.max(m2[1:], axis=0))
    out_ref[...] = jnp.where(lane_at < OWN, gains, best)


def local(features, labels, weights, nodes):
    dma = pltpu.SemaphoreType.DMA
    result = pl.pallas_call(
        kernel,
        out_shape=jax.ShapeDtypeStruct((8, 128), f32),
        in_specs=[pl.BlockSpec(memory_space=pl.ANY)] * 4,
        out_specs=pl.BlockSpec(memory_space=pltpu.VMEM),
        scratch_shapes=[
            pltpu.VMEM((512, LOCAL), f32),
            pltpu.VMEM((1, LOCAL), jnp.int32),
            pltpu.VMEM((1, LOCAL), bf16),
            pltpu.VMEM((1, LOCAL), jnp.int32),
            pltpu.VMEM((ROWS_AX, FEAT_AX + 1, 8, 128), bf16),
            pltpu.VMEM((ROWS_AX, FEAT_AX + 1, 8, 128), bf16),
            pltpu.VMEM((ROWS_AX, FEAT_AX, 2, 8, 128), bf16),
            pltpu.VMEM((OWN * B, NODES * C), f32),
            pltpu.VMEM((8, 128), f32),
            pltpu.VMEM((FEAT_AX, 8, 128), f32),
            pltpu.VMEM((8, 128), f32),
            pltpu.VMEM((ROWS_AX, 8, 128), f32),
            dma((4,)), dma(()), dma((ROWS_AX,)), dma(()), dma((ROWS_AX,)), dma(()), dma(()), dma(()), dma(()),
        ],
        compiler_params=pltpu.CompilerParams(collective_id=0, has_side_effects=True, vmem_limit_bytes=67043328),
        name="split_scores",
    )(features, labels.reshape(1, -1), weights, nodes)
    return result[None, :NODES, :OWN], result[:NODES, OWN][None]


def solution(mesh):
    return jax.shard_map(
        local,
        mesh=mesh,
        in_specs=(
            P(None, ("rows", "feat")),
            P(("rows", "feat")),
            P("leaf", ("rows", "feat")),
            P("leaf", ("rows", "feat")),
        ),
        out_specs=(P("leaf", None, ("rows", "feat")), P("leaf", None)),
        check_vma=False,
    )
```

time: 60.3 us -> 47.9 us (0.79)
  Pallas kernels: 55.3 us -> 44.4 us
  local copies, waits for them, and re-layouts: 4.14 us -> 2.62 us
    pallas_call x1, Pallas kernels: 55.3 us -> 44.4 us  [local(): pl.pallas_call(kernel, out_shape=jax.ShapeDtypeStruct((8, 128), f32), in_...]
    unnamed x10 -> x0, local copies, waits for them, and re-layouts: 4.14 us -> none
    slice x0 -> x1, local copies, waits for them, and re-layouts: none -> 1.38 us  [local(): return (result[None, :NODES, :OWN], result[:NODES, OWN][None])]
    broadcast_in_dim x0 -> x1, local copies, waits for them, and re-layouts: none -> 1.24 us  [local(): return (result[None, :NODES, :OWN], result[:NODES, OWN][None])]
where the time goes in v2:
time: 47.9 us; the launch traced here: 47.7 us
  Pallas kernels  44.4 us (93%)
  local copies, waits for them, and re-layouts  2.62 us (5%)
  between operations  0.64 us (1%)
    pallas_call x1, Pallas kernels, local(): pl.pallas_call(kernel, out_shape=jax.ShapeDtypeStruct((8, 128), f32), in_...  44.4 us
    slice x1, local copies, waits for them, and re-layouts, local(): return (result[None, :NODES, :OWN], result[:NODES, OWN][None])  1.38 us
    broadcast_in_dim x1, local copies, waits for them, and re-layouts, local(): return (result[None, :NODES, :OWN], result[:NODES, OWN][None])  1.24 us

profile of v2, /device:TPU:1, one launch (start us, length us, event | category | flops | bytes accessed | tf_op | source)
XLA Modules:
  0.0 47.7 jit_solution(11679819383218980021)
XLA Ops:
  0.6 44.4 %split_scores.1 = f32[8,128]{1,0:T(8,128)} custom-call(f32[512,256]{1,0:T(8,128)} %feat_hbm.1, s32[1,256]{1,0:T(1,128)} %bitcast.4, bf16[1,256]{1,0:T(2,128)(2,1)} %wei_hbm.1, s32[1,256]{1,0:T(1,128)} %node_hbm.1), custom_call_target="tpu_custom_call" | custom-call | tf_op jit(solution)/shard_map/split_scores/pallas_call | solution.py:224
  45.0 1.4 %slice_reduce_fusion = f32[2]{0:T(128)} fusion(f32[8,128]{1,0:T(8,128)} %split_scores.1), kind=kLoop, calls=%fused_computation | loop fusion | bytes 16 | tf_op jit(solution)/shard_map/slice | solution.py:247
  46.4 1.2 %slice_bitcast_fusion = f32[1,2,4]{2,1,0:T(2,128)} fusion(f32[8,128]{1,0:T(8,128)} %split_scores.1), kind=kLoop, calls=%fused_computation.1 | loop fusion | bytes 64 | tf_op jit(solution)/shard_map/broadcast_in_dim | solution.py:247

commit v3 on v2

--- a/solution.py
+++ b/solution.py
@@ -17,12 +17,13 @@
 FEAT_AX = X * CORES
 LOCAL = 256
 GROUP = 2
-AHEAD = 2
+AHEAD = 3
 f32 = jnp.float32
 bf16 = jnp.bfloat16
 MESH = pl.DeviceIdType.MESH
 NT = (((1,), (1,)), ((), ()))
 ORDER = [(0, 0), (0, 1), (1, 0), (7, 0), (1, 1), (7, 1), (2, 0), (6, 0), (2, 1), (6, 1), (3, 0), (5, 0), (3, 1), (5, 1), (4, 0), (4, 1)]
+LEVELS = [(1, 4), (4, 8), (8, 12), (12, 15), (15, 16)]
 
 
 def bin_index(x):
@@ -68,7 +69,7 @@
 def kernel(
     feat_hbm, lab_hbm, wei_hbm, node_hbm, out_ref,
     feat_v, lab_v, wei_v, node_v, send, zbuf, rbuf, acc, m1s, m1, m2s, m2,
-    in_sem, s1_send, s1_recv, s2_send, s2_recv, m1_send, m1_recv, m2_send, m2_recv,
+    relay, in_sem, s1_send, s1_recv, s2_send, s2_recv, m1_send, m1_recv, m2_send, m2_recv,
 ):
     my_rows, my_feat = lax.axis_index("rows"), lax.axis_index("feat")
     z, y = lax.div(my_rows, Y), lax.rem(my_rows, Y)
@@ -80,7 +81,7 @@
         return lax.rem(my_feat + d, FEAT_AX)
 
     barrier = pltpu.get_barrier_semaphore()
-    for dz, dy in reversed(ORDER[1:]):
+    for dz, dy in ORDER[slice(*LEVELS[0])]:
         pl.semaphore_signal(barrier, inc=1, device_id={"rows": rows_peer(dz, dy)}, device_id_type=MESH)
     for d in range(1, FEAT_AX):
         pl.semaphore_signal(barrier, inc=1, device_id={"feat": feat_peer(d)}, device_id_type=MESH)
@@ -126,14 +127,6 @@
     zbuf[0, :FEAT_AX] = binned(my_rows)
     zbuf[0, FEAT_AX] = codes
     acc[...] = jnp.zeros_like(acc)
-
-    pl.semaphore_wait(barrier, ROWS_AX - 1 + FEAT_AX - 1)
-
-    for s in range(1, ROWS_AX):
-        peer = rows_peer(*ORDER[s])
-        pltpu.make_async_remote_copy(
-            src_ref=send.at[peer], dst_ref=zbuf.at[s], send_sem=s1_send, recv_sem=s1_recv.at[s],
-            device_id={"rows": peer}, device_id_type=MESH).start()
 
     def forward(s, wait=True):
         if wait:
@@ -162,7 +155,24 @@
                 targets.append(target_tile(rbuf[s, d, 1].astype(f32), classes))
         acc[...] += lax.dot_general(jnp.concatenate(masks, axis=1), jnp.concatenate(targets, axis=1), NT, preferred_element_type=f32)
 
-    forward(0, wait=False)
+    def send_level(k):
+        for s in range(*LEVELS[k]):
+            peer = rows_peer(*ORDER[s])
+            pltpu.make_async_remote_copy(
+                src_ref=send.at[peer], dst_ref=zbuf.at[s], send_sem=s1_send, recv_sem=s1_recv.at[s],
+                device_id={"rows": peer}, device_id_type=MESH).start()
+
+    pl.semaphore_wait(barrier, LEVELS[0][1] - LEVELS[0][0] + FEAT_AX - 1)
+    for k in range(len(LEVELS)):
+        if k > 0:
+            for side in range(2):
+                pl.semaphore_wait(relay.at[k - 1, side], 1)
+        if k + 1 < len(LEVELS):
+            for side, dz in enumerate((1, Z - 1)):
+                pl.semaphore_signal(relay.at[k, side], inc=1, device_id={"rows": rows_peer(dz, 0)}, device_id_type=MESH)
+        send_level(k)
+        if k == 0:
+            forward(0, wait=False)
     for s in range(1, AHEAD * GROUP):
         forward(s)
 
@@ -239,11 +249,12 @@
             pltpu.VMEM((FEAT_AX, 8, 128), f32),
             pltpu.VMEM((8, 128), f32),
             pltpu.VMEM((ROWS_AX, 8, 128), f32),
+            pltpu.SemaphoreType.REGULAR((len(LEVELS) - 1, 2)),
             dma((4,)), dma(()), dma((ROWS_AX,)), dma(()), dma((ROWS_AX,)), dma(()), dma(()), dma(()), dma(()),
         ],
-        compiler_params=pltpu.CompilerParams(collective_id=0, has_side_effects=True, vmem_limit_bytes=67043328),
+        compiler_params=pltpu.CompilerParams(collective_id=0, has_side_effects=True, vmem_limit_bytes=48 * 1024 * 1024),
         name="split_scores",
-    )(features, labels.reshape(1, -1), weights, nodes)
+    )(*[pltpu.with_memory_space_constraint(v, pltpu.HBM) for v in (features, labels.reshape(1, -1), weights, nodes)])
     return result[None, :NODES, :OWN], result[:NODES, OWN][None]
 
 

time: 47.9 us -> 43.4 us (0.906)
  Pallas kernels: 44.4 us -> 41.3 us
  local copies, waits for them, and re-layouts: 2.62 us -> 1.26 us
    pallas_call x1, Pallas kernels: 44.4 us -> 41.3 us  [local(): pl.pallas_call(kernel, out_shape=jax.ShapeDtypeStruct((8, 128), f32), in_...]
    slice x1, local copies, waits for them, and re-layouts: 1.38 us -> 0.69 us  [local(): return (result[None, :NODES, :OWN], result[:NODES, OWN][None])]
    broadcast_in_dim x1, local copies, waits for them, and re-layouts: 1.24 us -> 0.56 us  [local(): return (result[None, :NODES, :OWN], result[:NODES, OWN][None])]
where the time goes in v3:
time: 43.4 us; the launch traced here: 43.2 us
  Pallas kernels  41.3 us (95%)
  local copies, waits for them, and re-layouts  1.26 us (3%)
  between operations  0.64 us (1%)
    pallas_call x1, Pallas kernels, local(): pl.pallas_call(kernel, out_shape=jax.ShapeDtypeStruct((8, 128), f32), in_...  41.3 us

profile of v3, /device:TPU:1, one launch (start us, length us, event | category | flops | bytes accessed | tf_op | source)
XLA Modules:
  0.0 43.2 jit_solution(11283868194830575594)
XLA Ops:
  0.6 41.3 %split_scores.1 = f32[8,128]{1,0:T(8,128)S(1)} custom-call(f32[512,256]{1,0:T(8,128)} %feat_hbm.1, s32[1,256]{1,0:T(1,128)} %bitcast.4, bf16[1,256]{1,0:T(2,128)(2,1)} %wei_hbm.1, s32[1,256]{1,0:T(1,128)} %node_hbm.1), custom_call_target="tpu_custom_call" | custom-call | tf_op jit(solution)/shard_map/split_scores/pallas_call | solution.py:234
  42.0 0.7 %slice_reduce_fusion = f32[2]{0:T(128)} fusion(f32[8,128]{1,0:T(8,128)S(1)} %split_scores.1), kind=kLoop, calls=%fused_computation | loop fusion | bytes 16 | tf_op jit(solution)/shard_map/slice | solution.py:258
  42.7 0.6 %slice_bitcast_fusion = f32[1,2,4]{2,1,0:T(2,128)} fusion(f32[8,128]{1,0:T(8,128)S(1)} %split_scores.1), kind=kLoop, calls=%fused_computation.1 | loop fusion | bytes 64 | tf_op jit(solution)/shard_map/broadcast_in_dim | solution.py:258

commit v4 on v3

--- a/solution.py
+++ b/solution.py
@@ -14,10 +14,9 @@
 X = 4
 CORES = 2
 ROWS_AX = Z * Y
+CHUNKS = 4
 FEAT_AX = X * CORES
 LOCAL = 256
-GROUP = 2
-AHEAD = 3
 f32 = jnp.float32
 bf16 = jnp.bfloat16
 MESH = pl.DeviceIdType.MESH
@@ -87,12 +86,15 @@
         pl.semaphore_signal(barrier, inc=1, device_id={"feat": feat_peer(d)}, device_id_type=MESH)
 
     loads = [
-        pltpu.make_async_copy(feat_hbm, feat_v, in_sem.at[0]),
-        pltpu.make_async_copy(lab_hbm, lab_v, in_sem.at[1]),
-        pltpu.make_async_copy(wei_hbm, wei_v, in_sem.at[2]),
-        pltpu.make_async_copy(node_hbm, node_v, in_sem.at[3]),
+        pltpu.make_async_copy(lab_hbm, lab_v, in_sem.at[CHUNKS]),
+        pltpu.make_async_copy(wei_hbm, wei_v, in_sem.at[CHUNKS + 1]),
+        pltpu.make_async_copy(node_hbm, node_v, in_sem.at[CHUNKS + 2]),
     ]
-    for load in loads:
+    chunk_loads = []
+    for q in range(CHUNKS):
+        part = pl.ds(q * (512 // CHUNKS), 512 // CHUNKS)
+        chunk_loads.append(pltpu.make_async_copy(feat_hbm.at[part], feat_v.at[part], in_sem.at[q]))
+    for load in loads + chunk_loads:
         load.start()
     for load in loads:
         load.wait()
@@ -123,7 +125,9 @@
         send[r, FEAT_AX] = codes
         return carry
 
-    lax.fori_loop(0, ROWS_AX, place, 0)
+    for q in range(CHUNKS):
+        chunk_loads[q].wait()
+        lax.fori_loop(q * (ROWS_AX // CHUNKS), (q + 1) * (ROWS_AX // CHUNKS), place, 0)
     zbuf[0, :FEAT_AX] = binned(my_rows)
     zbuf[0, FEAT_AX] = codes
     acc[...] = jnp.zeros_like(acc)
@@ -141,13 +145,13 @@
     bins = (lax.broadcasted_iota(jnp.int32, (8, 16, 128), 0) * 16 + lax.broadcasted_iota(jnp.int32, (8, 16, 128), 1)).astype(f32).astype(bf16)
     classes = bins[: C // 16]
 
-    def use(g):
+    def use(start, count):
         masks, targets = [], []
-        for u in range(GROUP):
-            part = rbuf.at[g * GROUP + u, pl.ds(1, FEAT_AX - 1)]
-            pltpu.make_async_copy(part, part, s2_recv.at[g * GROUP + u]).wait()
-        for u in range(GROUP):
-            s = g * GROUP + u
+        for u in range(count):
+            part = rbuf.at[start + u, pl.ds(1, FEAT_AX - 1)]
+            pltpu.make_async_copy(part, part, s2_recv.at[start + u]).wait()
+        for u in range(count):
+            s = start + u
             masks.append(mask_tile(zbuf[s, my_feat].astype(f32), bins))
             targets.append(target_tile(zbuf[s, FEAT_AX].astype(f32), classes))
             for d in range(1, FEAT_AX):
@@ -162,8 +166,7 @@
                 src_ref=send.at[peer], dst_ref=zbuf.at[s], send_sem=s1_send, recv_sem=s1_recv.at[s],
                 device_id={"rows": peer}, device_id_type=MESH).start()
 
-    pl.semaphore_wait(barrier, LEVELS[0][1] - LEVELS[0][0] + FEAT_AX - 1)
-    for k in range(len(LEVELS)):
+    def level(k):
         if k > 0:
             for side in range(2):
                 pl.semaphore_wait(relay.at[k - 1, side], 1)
@@ -171,29 +174,46 @@
             for side, dz in enumerate((1, Z - 1)):
                 pl.semaphore_signal(relay.at[k, side], inc=1, device_id={"rows": rows_peer(dz, 0)}, device_id_type=MESH)
         send_level(k)
-        if k == 0:
-            forward(0, wait=False)
-    for s in range(1, AHEAD * GROUP):
-        forward(s)
+
+    def forward_all(first, last):
+        for s in range(first, last):
+            forward(s, wait=s > 0)
+
+    pl.semaphore_wait(barrier, LEVELS[0][1] - LEVELS[0][0] + FEAT_AX - 1)
+    level(0)
+    forward_all(0, 1)
+    level(1)
+    forward_all(1, 4)
+    level(2)
+    use(0, 1)
+    level(3)
+    forward_all(4, 8)
 
     def step(g, carry):
-        for u in range(GROUP):
-            forward((g + AHEAD) * GROUP + u)
-        use(g)
+        @pl.when(g == 1)
+        def _():
+            level(4)
+            forward_all(8, 12)
+
+        @pl.when(g == 2)
+        def _():
+            forward_all(12, 15)
+
+        @pl.when(g == 3)
+        def _():
+            forward_all(15, 16)
+
+        use(1 + 2 * g, 2)
         return carry
 
-    def tail(g, carry):
-        use(g)
-        return carry
-
-    steps = ROWS_AX // GROUP
-    lax.fori_loop(0, steps - AHEAD, step, 0)
-    lax.fori_loop(steps - AHEAD, steps, tail, 0)
+    lax.fori_loop(0, 7, step, 0)
+    use(15, 1)
 
     row_at = lax.broadcasted_iota(jnp.int32, (8, 128), 0)
     lane_at = lax.broadcasted_iota(jnp.int32, (8, 128), 1)
     gains = jnp.zeros((8, 128), f32)
-    best = jnp.zeros((8, 128), f32)
+    best = jnp.zeros((1, 128), f32)
+    lane_row = lax.broadcasted_iota(jnp.int32, (1, 128), 1)
     for n in range(NODES):
         node_top = None
         for i in range(OWN):
@@ -204,7 +224,7 @@
             top = jnp.max(gain, axis=1, keepdims=True)
             gains = jnp.where((row_at == n) & (lane_at == i), top, gains)
             node_top = top if node_top is None else jnp.maximum(node_top, top)
-        best = jnp.where(row_at == n, node_top, best)
+        best = jnp.where(lane_row == n, node_top, best)
 
     m1s[...] = best
     for d in range(1, FEAT_AX):
@@ -226,7 +246,8 @@
     pltpu.make_async_copy(m2_all, m2_all, m2_send).wait()
     pltpu.make_async_copy(m2_all, m2_all, m2_recv).wait()
     best = jnp.maximum(best, jnp.max(m2[1:], axis=0))
-    out_ref[...] = jnp.where(lane_at < OWN, gains, best)
+    best_column = jnp.where(row_at == 0, best[:, 0:1], best[:, 1:2])
+    out_ref[...] = jnp.where(lane_at < OWN, gains, best_column)
 
 
 def local(features, labels, weights, nodes):
@@ -245,12 +266,12 @@
             pltpu.VMEM((ROWS_AX, FEAT_AX + 1, 8, 128), bf16),
             pltpu.VMEM((ROWS_AX, FEAT_AX, 2, 8, 128), bf16),
             pltpu.VMEM((OWN * B, NODES * C), f32),
-            pltpu.VMEM((8, 128), f32),
-            pltpu.VMEM((FEAT_AX, 8, 128), f32),
-            pltpu.VMEM((8, 128), f32),
-            pltpu.VMEM((ROWS_AX, 8, 128), f32),
+            pltpu.VMEM((1, 128), f32),
+            pltpu.VMEM((FEAT_AX, 1, 128), f32),
+            pltpu.VMEM((1, 128), f32),
+            pltpu.VMEM((ROWS_AX, 1, 128), f32),
             pltpu.SemaphoreType.REGULAR((len(LEVELS) - 1, 2)),
-            dma((4,)), dma(()), dma((ROWS_AX,)), dma(()), dma((ROWS_AX,)), dma(()), dma(()), dma(()), dma(()),
+            dma((CHUNKS + 3,)), dma(()), dma((ROWS_AX,)), dma(()), dma((ROWS_AX,)), dma(()), dma(()), dma(()), dma(()),
         ],
         compiler_params=pltpu.CompilerParams(collective_id=0, has_side_effects=True, vmem_limit_bytes=48 * 1024 * 1024),
         name="split_scores",

time: 43.4 us -> 41.9 us (0.965)
  Pallas kernels: 41.3 us -> 39.7 us
    pallas_call x1, Pallas kernels: 41.3 us -> 39.7 us  [local(): pl.pallas_call(kernel, out_shape=jax.ShapeDtypeStruct((8, 128), f32), in_...]
where the time goes in v4:
time: 41.9 us; the launch traced here: 41.6 us
  Pallas kernels  39.7 us (95%)
  local copies, waits for them, and re-layouts  1.26 us (3%)
  between operations  0.64 us (2%)
    pallas_call x1, Pallas kernels, local(): pl.pallas_call(kernel, out_shape=jax.ShapeDtypeStruct((8, 128), f32), in_...  39.7 us

profile of v4, /device:TPU:1, one launch (start us, length us, event | category | flops | bytes accessed | tf_op | source)
XLA Modules:
  0.0 41.6 jit_solution(18180476228363396179)
XLA Ops:
  0.6 39.7 %split_scores.1 = f32[8,128]{1,0:T(8,128)S(1)} custom-call(f32[512,256]{1,0:T(8,128)} %feat_hbm.1, s32[1,256]{1,0:T(1,128)} %bitcast.4, bf16[1,256]{1,0:T(2,128)(2,1)} %wei_hbm.1, s32[1,256]{1,0:T(1,128)} %node_hbm.1), custom_call_target="tpu_custom_call" | custom-call | tf_op jit(solution)/shard_map/split_scores/pallas_call | solution.py:255
  40.3 0.7 %slice_reduce_fusion = f32[2]{0:T(128)} fusion(f32[8,128]{1,0:T(8,128)S(1)} %split_scores.1), kind=kLoop, calls=%fused_computation | loop fusion | bytes 16 | tf_op jit(solution)/shard_map/slice | solution.py:279
  41.0 0.6 %slice_bitcast_fusion = f32[1,2,4]{2,1,0:T(2,128)} fusion(f32[8,128]{1,0:T(8,128)S(1)} %split_scores.1), kind=kLoop, calls=%fused_computation.1 | loop fusion | bytes 64 | tf_op jit(solution)/shard_map/broadcast_in_dim | solution.py:279

commit v5 on v4

--- a/solution.py
+++ b/solution.py
@@ -22,7 +22,7 @@
 MESH = pl.DeviceIdType.MESH
 NT = (((1,), (1,)), ((), ()))
 ORDER = [(0, 0), (0, 1), (1, 0), (7, 0), (1, 1), (7, 1), (2, 0), (6, 0), (2, 1), (6, 1), (3, 0), (5, 0), (3, 1), (5, 1), (4, 0), (4, 1)]
-LEVELS = [(1, 4), (4, 8), (8, 12), (12, 15), (15, 16)]
+LEVELS = [(1, 6), (6, 10), (10, 16)]
 
 
 def bin_index(x):
@@ -166,42 +166,36 @@
                 src_ref=send.at[peer], dst_ref=zbuf.at[s], send_sem=s1_send, recv_sem=s1_recv.at[s],
                 device_id={"rows": peer}, device_id_type=MESH).start()
 
-    def level(k):
-        if k > 0:
-            for side in range(2):
-                pl.semaphore_wait(relay.at[k - 1, side], 1)
-        if k + 1 < len(LEVELS):
-            for side, dz in enumerate((1, Z - 1)):
-                pl.semaphore_signal(relay.at[k, side], inc=1, device_id={"rows": rows_peer(dz, 0)}, device_id_type=MESH)
-        send_level(k)
+    def tell(k, side):
+        peer = rows_peer(((k + 1) if side == 0 else (Z - 1 - k)), 0)
+        pl.semaphore_signal(relay.at[k, side], inc=1, device_id={"rows": peer}, device_id_type=MESH)
 
     def forward_all(first, last):
         for s in range(first, last):
             forward(s, wait=s > 0)
 
     pl.semaphore_wait(barrier, LEVELS[0][1] - LEVELS[0][0] + FEAT_AX - 1)
-    level(0)
+    for side in range(2):
+        tell(0, side)
+    send_level(0)
     forward_all(0, 1)
-    level(1)
+    for side in range(2):
+        pl.semaphore_wait(relay.at[0, side], 1)
+    for side in range(2):
+        tell(1, side)
+    send_level(1)
     forward_all(1, 4)
-    level(2)
     use(0, 1)
-    level(3)
-    forward_all(4, 8)
+    for side in range(2):
+        pl.semaphore_wait(relay.at[1, side], 1)
+    send_level(2)
+    forward_all(4, 6)
 
     def step(g, carry):
-        @pl.when(g == 1)
+        @pl.when(g < 5)
         def _():
-            level(4)
-            forward_all(8, 12)
-
-        @pl.when(g == 2)
-        def _():
-            forward_all(12, 15)
-
-        @pl.when(g == 3)
-        def _():
-            forward_all(15, 16)
+            forward(6 + 2 * g)
+            forward(7 + 2 * g)
 
         use(1 + 2 * g, 2)
         return carry

time: 41.9 us -> 41 us (0.979)
  Pallas kernels: 39.7 us -> 38.9 us
    pallas_call x1, Pallas kernels: 39.7 us -> 38.9 us  [local(): pl.pallas_call(kernel, out_shape=jax.ShapeDtypeStruct((8, 128), f32), in_...]
where the time goes in v5:
time: 41 us; the launch traced here: 40.8 us
  Pallas kernels  38.9 us (95%)
  local copies, waits for them, and re-layouts  1.26 us (3%)
  between operations  0.64 us (2%)
    pallas_call x1, Pallas kernels, local(): pl.pallas_call(kernel, out_shape=jax.ShapeDtypeStruct((8, 128), f32), in_...  38.9 us

profile of v5, /device:TPU:1, one launch (start us, length us, event | category | flops | bytes accessed | tf_op | source)
XLA Modules:
  0.0 40.8 jit_solution(6221237700145919768)
XLA Ops:
  0.6 38.9 %split_scores.1 = f32[8,128]{1,0:T(8,128)S(1)} custom-call(f32[512,256]{1,0:T(8,128)} %feat_hbm.1, s32[1,256]{1,0:T(1,128)} %bitcast.4, bf16[1,256]{1,0:T(2,128)(2,1)} %wei_hbm.1, s32[1,256]{1,0:T(1,128)} %node_hbm.1), custom_call_target="tpu_custom_call" | custom-call | tf_op jit(solution)/shard_map/split_scores/pallas_call | solution.py:249
  39.5 0.7 %slice_reduce_fusion = f32[2]{0:T(128)} fusion(f32[8,128]{1,0:T(8,128)S(1)} %split_scores.1), kind=kLoop, calls=%fused_computation | loop fusion | bytes 16 | tf_op jit(solution)/shard_map/slice | solution.py:273
  40.2 0.6 %slice_bitcast_fusion = f32[1,2,4]{2,1,0:T(2,128)} fusion(f32[8,128]{1,0:T(8,128)S(1)} %split_scores.1), kind=kLoop, calls=%fused_computation.1 | loop fusion | bytes 64 | tf_op jit(solution)/shard_map/broadcast_in_dim | solution.py:273

commit v6 on v5

--- a/solution.py
+++ b/solution.py
@@ -22,7 +22,8 @@
 MESH = pl.DeviceIdType.MESH
 NT = (((1,), (1,)), ((), ()))
 ORDER = [(0, 0), (0, 1), (1, 0), (7, 0), (1, 1), (7, 1), (2, 0), (6, 0), (2, 1), (6, 1), (3, 0), (5, 0), (3, 1), (5, 1), (4, 0), (4, 1)]
-LEVELS = [(1, 6), (6, 10), (10, 16)]
+LEVELS = [(4, 6), (6, 10), (10, 16)]
+DIRECT = (1, 4)
 
 
 def bin_index(x):
@@ -68,7 +69,7 @@
 def kernel(
     feat_hbm, lab_hbm, wei_hbm, node_hbm, out_ref,
     feat_v, lab_v, wei_v, node_v, send, zbuf, rbuf, acc, m1s, m1, m2s, m2,
-    relay, in_sem, s1_send, s1_recv, s2_send, s2_recv, m1_send, m1_recv, m2_send, m2_recv,
+    relay, in_sem, s0_send, s1_send, s1_recv, s2_send, s2_recv, m1_send, m1_recv, m2_send, m2_recv,
 ):
     my_rows, my_feat = lax.axis_index("rows"), lax.axis_index("feat")
     z, y = lax.div(my_rows, Y), lax.rem(my_rows, Y)
@@ -80,10 +81,12 @@
         return lax.rem(my_feat + d, FEAT_AX)
 
     barrier = pltpu.get_barrier_semaphore()
-    for dz, dy in ORDER[slice(*LEVELS[0])]:
+    for dz, dy in ORDER[LEVELS[0][0] : LEVELS[0][1]]:
         pl.semaphore_signal(barrier, inc=1, device_id={"rows": rows_peer(dz, dy)}, device_id_type=MESH)
-    for d in range(1, FEAT_AX):
-        pl.semaphore_signal(barrier, inc=1, device_id={"feat": feat_peer(d)}, device_id_type=MESH)
+    for dz, dy in ORDER[: DIRECT[1]]:
+        for d in range(FEAT_AX):
+            if (dz, dy, d) != (0, 0, 0):
+                pl.semaphore_signal(barrier, inc=1, device_id={"rows": rows_peer(dz, dy), "feat": feat_peer(d)}, device_id_type=MESH)
 
     loads = [
         pltpu.make_async_copy(lab_hbm, lab_v, in_sem.at[CHUNKS]),
@@ -170,26 +173,36 @@
         peer = rows_peer(((k + 1) if side == 0 else (Z - 1 - k)), 0)
         pl.semaphore_signal(relay.at[k, side], inc=1, device_id={"rows": peer}, device_id_type=MESH)
 
-    def forward_all(first, last):
-        for s in range(first, last):
-            forward(s, wait=s > 0)
-
-    pl.semaphore_wait(barrier, LEVELS[0][1] - LEVELS[0][0] + FEAT_AX - 1)
+    pl.semaphore_wait(barrier, LEVELS[0][1] - LEVELS[0][0] + DIRECT[1] * FEAT_AX - 1)
     for side in range(2):
         tell(0, side)
+    for s in range(*DIRECT):
+        rows = rows_peer(*ORDER[s])
+        for d in range(FEAT_AX):
+            feat = feat_peer(d)
+            for part, block in ((0, feat), (1, FEAT_AX)):
+                pltpu.make_async_remote_copy(
+                    src_ref=send.at[rows, block],
+                    dst_ref=zbuf.at[s, block] if d == 0 else rbuf.at[s, d, part],
+                    send_sem=s0_send if d == 0 else s2_send,
+                    recv_sem=s1_recv.at[s] if d == 0 else s2_recv.at[s],
+                    device_id={"rows": rows, "feat": feat}, device_id_type=MESH).start()
+    forward(0, wait=False)
     send_level(0)
-    forward_all(0, 1)
     for side in range(2):
         pl.semaphore_wait(relay.at[0, side], 1)
     for side in range(2):
         tell(1, side)
     send_level(1)
-    forward_all(1, 4)
-    use(0, 1)
     for side in range(2):
         pl.semaphore_wait(relay.at[1, side], 1)
     send_level(2)
-    forward_all(4, 6)
+    forward(4)
+    forward(5)
+    use(0, 1)
+    for s in range(*DIRECT):
+        part = zbuf.at[s, pl.ds(0, 2)]
+        pltpu.make_async_copy(part, part, s1_recv.at[s]).wait()
 
     def step(g, carry):
         @pl.when(g < 5)
@@ -233,7 +246,9 @@
         pltpu.make_async_remote_copy(
             src_ref=m2s, dst_ref=m2.at[s], send_sem=m2_send, recv_sem=m2_recv,
             device_id={"rows": rows_peer(*ORDER[s])}, device_id_type=MESH).start()
-    z_all, r_all = zbuf.at[pl.ds(1, ROWS_AX - 1)], rbuf.at[:, pl.ds(1, FEAT_AX - 1)]
+    z_near, z_all = zbuf.at[pl.ds(DIRECT[0], DIRECT[1] - DIRECT[0]), pl.ds(0, 2)], zbuf.at[pl.ds(DIRECT[1], ROWS_AX - DIRECT[1])]
+    r_all = rbuf.at[:, pl.ds(1, FEAT_AX - 1)]
+    pltpu.make_async_copy(z_near, z_near, s0_send).wait()
     pltpu.make_async_copy(z_all, z_all, s1_send).wait()
     pltpu.make_async_copy(r_all, r_all, s2_send).wait()
     pltpu.make_async_copy(m1_all, m1_all, m1_send).wait()
@@ -265,12 +280,12 @@
             pltpu.VMEM((1, 128), f32),
             pltpu.VMEM((ROWS_AX, 1, 128), f32),
             pltpu.SemaphoreType.REGULAR((len(LEVELS) - 1, 2)),
-            dma((CHUNKS + 3,)), dma(()), dma((ROWS_AX,)), dma(()), dma((ROWS_AX,)), dma(()), dma(()), dma(()), dma(()),
+            dma((CHUNKS + 3,)), dma(()), dma(()), dma((ROWS_AX,)), dma(()), dma((ROWS_AX,)), dma(()), dma(()), dma(()), dma(()),
         ],
         compiler_params=pltpu.CompilerParams(collective_id=0, has_side_effects=True, vmem_limit_bytes=48 * 1024 * 1024),
         name="split_scores",
     )(*[pltpu.with_memory_space_constraint(v, pltpu.HBM) for v in (features, labels.reshape(1, -1), weights, nodes)])
-    return result[None, :NODES, :OWN], result[:NODES, OWN][None]
+    return result[None, :NODES, :OWN], jnp.max(result[None, :NODES, OWN : 2 * OWN], axis=2)
 
 
 def solution(mesh):

time: 41 us -> 41.4 us (level)
  local copies, waits for them, and re-layouts: 1.26 us -> 0 us
  other arithmetic: 0 us -> 1.19 us
  Pallas kernels: 38.9 us -> 39.4 us
    reduce_max x0 -> x1, other arithmetic: none -> 1.19 us  [local(): jnp.max(result[None, :NODES, OWN:2 * OWN], axis=2)]
    slice x1 -> x0, local copies, waits for them, and re-layouts: 0.69 us -> none  [local(): return (result[None, :NODES, :OWN], result[:NODES, OWN][None])]
    broadcast_in_dim x1 -> x0, local copies, waits for them, and re-layouts: 0.56 us -> none  [local(): return (result[None, :NODES, :OWN], result[:NODES, OWN][None])]
    pallas_call x1, Pallas kernels: 38.9 us -> 39.4 us  [local(): pl.pallas_call(kernel, out_shape=jax.ShapeDtypeStruct((8, 128), f32), in_...]
where the time goes in v6:
time: 41.4 us; the launch traced here: 41.2 us
  Pallas kernels  39.4 us (95%)
  other arithmetic  1.19 us (3%)
  between operations  0.64 us (2%)
    pallas_call x1, Pallas kernels, local(): pl.pallas_call(kernel, out_shape=jax.ShapeDtypeStruct((8, 128), f32), in_...  39.4 us
    reduce_max x1, other arithmetic, local(): jnp.max(result[None, :NODES, OWN:2 * OWN], axis=2)  1.19 us

profile of v6, /device:TPU:1, one launch (start us, length us, event | category | flops | bytes accessed | tf_op | source)
XLA Modules:
  0.0 41.2 jit_solution(13715895874858527685)
XLA Ops:
  0.6 39.4 %split_scores.1 = f32[8,128]{1,0:T(8,128)S(1)} custom-call(f32[512,256]{1,0:T(8,128)} %feat_hbm.1, s32[1,256]{1,0:T(1,128)} %bitcast.4, bf16[1,256]{1,0:T(2,128)(2,1)} %wei_hbm.1, s32[1,256]{1,0:T(1,128)} %node_hbm.1), custom_call_target="tpu_custom_call" | custom-call | tf_op jit(solution)/shard_map/split_scores/pallas_call | solution.py:264
  40.0 1.2 %slice_reduce_fusion = (f32[2]{0:T(128)}, f32[1,2,4]{2,1,0:T(2,128)}) fusion(f32[8,128]{1,0:T(8,128)S(1)} %split_scores.1), kind=kLoop, calls=%fused_computation | loop fusion | flops 6 | bytes 104 | tf_op jit(solution)/shard_map/reduce_max | solution.py:288

commit v7 on v5

--- a/solution.py
+++ b/solution.py
@@ -184,11 +184,11 @@
     for side in range(2):
         tell(1, side)
     send_level(1)
+    for side in range(2):
+        pl.semaphore_wait(relay.at[1, side], 1)
+    send_level(2)
     forward_all(1, 4)
     use(0, 1)
-    for side in range(2):
-        pl.semaphore_wait(relay.at[1, side], 1)
-    send_level(2)
     forward_all(4, 6)
 
     def step(g, carry):
@@ -270,7 +270,7 @@
         compiler_params=pltpu.CompilerParams(collective_id=0, has_side_effects=True, vmem_limit_bytes=48 * 1024 * 1024),
         name="split_scores",
     )(*[pltpu.with_memory_space_constraint(v, pltpu.HBM) for v in (features, labels.reshape(1, -1), weights, nodes)])
-    return result[None, :NODES, :OWN], result[:NODES, OWN][None]
+    return result[None, :NODES, :OWN], jnp.max(result[None, :NODES, OWN : 2 * OWN], axis=2)
 
 
 def solution(mesh):

time: 41 us -> 41.4 us (level)
  local copies, waits for them, and re-layouts: 1.26 us -> 0 us
  other arithmetic: 0 us -> 1.19 us
    reduce_max x0 -> x1, other arithmetic: none -> 1.19 us  [local(): jnp.max(result[None, :NODES, OWN:2 * OWN], axis=2)]
    slice x1 -> x0, local copies, waits for them, and re-layouts: 0.69 us -> none  [local(): return (result[None, :NODES, :OWN], result[:NODES, OWN][None])]
    broadcast_in_dim x1 -> x0, local copies, waits for them, and re-layouts: 0.56 us -> none  [local(): return (result[None, :NODES, :OWN], result[:NODES, OWN][None])]
    pallas_call x1, Pallas kernels: 38.9 us -> 39.3 us  [local(): pl.pallas_call(kernel, out_shape=jax.ShapeDtypeStruct((8, 128), f32), in_...]
where the time goes in v7:
time: 41.4 us; the launch traced here: 41.2 us
  Pallas kernels  39.3 us (95%)
  other arithmetic  1.19 us (3%)
  between operations  0.64 us (2%)
    pallas_call x1, Pallas kernels, local(): pl.pallas_call(kernel, out_shape=jax.ShapeDtypeStruct((8, 128), f32), in_...  39.3 us
    reduce_max x1, other arithmetic, local(): jnp.max(result[None, :NODES, OWN:2 * OWN], axis=2)  1.19 us

profile of v7, /device:TPU:1, one launch (start us, length us, event | category | flops | bytes accessed | tf_op | source)
XLA Modules:
  0.0 41.2 jit_solution(100109998995464852)
XLA Ops:
  0.6 39.3 %split_scores.1 = f32[8,128]{1,0:T(8,128)S(1)} custom-call(f32[512,256]{1,0:T(8,128)} %feat_hbm.1, s32[1,256]{1,0:T(1,128)} %bitcast.4, bf16[1,256]{1,0:T(2,128)(2,1)} %wei_hbm.1, s32[1,256]{1,0:T(1,128)} %node_hbm.1), custom_call_target="tpu_custom_call" | custom-call | tf_op jit(solution)/shard_map/split_scores/pallas_call | solution.py:249
  40.0 1.2 %slice_reduce_fusion = (f32[2]{0:T(128)}, f32[1,2,4]{2,1,0:T(2,128)}) fusion(f32[8,128]{1,0:T(8,128)S(1)} %split_scores.1), kind=kLoop, calls=%fused_computation | loop fusion | flops 6 | bytes 104 | tf_op jit(solution)/shard_map/reduce_max | solution.py:273

commit v8 on v7

v8 whole, which is shorter than its diff:
```python
import jax
import jax.numpy as jnp
from jax import lax
from jax.experimental import pallas as pl
from jax.experimental.pallas import tpu as pltpu
from jax.sharding import PartitionSpec as P

B = 128
C = 64
NODES = 2
OWN = 4
Z = 8
Y = 2
X = 4
CORES = 2
ROWS_AX = Z * Y
CHUNKS = 4
FEAT_AX = X * CORES
LOCAL = 256
f32 = jnp.float32
bf16 = jnp.bfloat16
MESH = pl.DeviceIdType.MESH
NT = (((1,), (1,)), ((), ()))
ORDER = [(0, 0), (0, 1), (1, 0), (7, 0), (1, 1), (7, 1), (2, 0), (6, 0), (2, 1), (6, 1), (3, 0), (5, 0), (3, 1), (5, 1), (4, 0), (4, 1)]
NEAR = 6


def bin_index(x):
    guess = jnp.clip(jnp.ceil(x * (B / 9.0) + (B // 2 - 1)), 0.0, B - 1.0)
    edge_here = (guess + (1.0 - B // 2)) * (9.0 / B)
    edge_before = (guess - (1.0 * (B // 2))) * (9.0 / B)
    up = jnp.where((edge_here < x) & (guess < B - 1.0), 1.0, 0.0)
    down = jnp.where((edge_before >= x) & (guess > 0.0), 1.0, 0.0)
    return guess + up - down


def row_pack(tile, row):
    return jnp.broadcast_to(tile[row : row + 1, :], (16, 128)).astype(bf16)


def mask_tile(tile, bins):
    one, zero = jnp.ones((), bf16), jnp.zeros((), bf16)
    rows = []
    for i in range(OWN):
        halves = []
        for h in range(2):
            packed = row_pack(tile, h * 4 + i)
            halves.append(jnp.where(packed[None] <= bins, one, zero).reshape(B, 128))
        rows.append(jnp.concatenate(halves, axis=1))
    return jnp.concatenate(rows, axis=0)


def target_tile(tile, classes):
    zero = jnp.zeros((), bf16)
    parts = [[], []]
    for h in range(2):
        hit = row_pack(tile, h * 4)[None] == classes
        for n in range(NODES):
            weight = jnp.broadcast_to(row_pack(tile, h * 4 + 1 + n)[None], hit.shape)
            parts[n].append(jnp.where(hit, weight, zero).reshape(C, 128))
    return jnp.concatenate([jnp.concatenate(p, axis=1) for p in parts], axis=0)


def ratio(values):
    return jnp.sum(values * values, axis=0, keepdims=True) / jnp.maximum(jnp.sum(values, axis=0, keepdims=True), 1.0)


def kernel(
    feat_hbm, lab_hbm, wei_hbm, node_hbm, out_ref,
    feat_v, lab_v, wei_v, node_v, send, own_codes, rbuf, acc, top_row, tops,
    in_sem, feat_recv, code_recv, far_recv, top_recv, sent,
):
    my_rows, my_feat = lax.axis_index("rows"), lax.axis_index("feat")
    z, y = lax.div(my_rows, Y), lax.rem(my_rows, Y)

    def rows_peer(s):
        dz, dy = ORDER[s]
        return lax.rem(z + dz, Z) * Y + lax.rem(y + dy, Y)

    def feat_peer(d):
        return lax.rem(my_feat + d, FEAT_AX)

    def to_column(s, action):
        rows = rows_peer(s)

        def one(d, carry):
            action(rows, feat_peer(d), d)
            return carry

        lax.fori_loop(1 if s == 0 else 0, FEAT_AX, one, 0)

    def push(source, target, send_sem, recv_sem, rows, feat):
        pltpu.make_async_remote_copy(
            src_ref=source, dst_ref=target, send_sem=send_sem, recv_sem=recv_sem,
            device_id={"rows": rows, "feat": feat}, device_id_type=MESH).start()

    def wait_all(part, sem):
        pltpu.make_async_copy(part, part, sem).wait()

    loads = [
        pltpu.make_async_copy(lab_hbm, lab_v, in_sem.at[CHUNKS]),
        pltpu.make_async_copy(wei_hbm, wei_v, in_sem.at[CHUNKS + 1]),
        pltpu.make_async_copy(node_hbm, node_v, in_sem.at[CHUNKS + 2]),
    ]
    chunk_loads = []
    for q in range(CHUNKS):
        part = pl.ds(q * (512 // CHUNKS), 512 // CHUNKS)
        chunk_loads.append(pltpu.make_async_copy(feat_hbm.at[part], feat_v.at[part], in_sem.at[q]))
    for load in loads + chunk_loads:
        load.start()

    barrier = pltpu.get_barrier_semaphore()

    def greet(rows, feat, d):
        pl.semaphore_signal(barrier, inc=1, device_id={"rows": rows, "feat": feat}, device_id_type=MESH)

    for s in reversed(range(ROWS_AX)):
        to_column(s, greet)
    for load in loads:
        load.wait()

    label = lab_v[...].astype(f32)
    weight = wei_v[...].astype(f32)
    node = node_v[...]
    w0 = jnp.where(node == 0, weight, 0.0)
    w1 = jnp.where(node == 1, weight, 0.0)
    pad = jnp.zeros_like(w0)
    lines = []
    for h in range(2):
        cut = slice(h * 128, (h + 1) * 128)
        lines += [label[:, cut], w0[:, cut], w1[:, cut], pad[:, cut]]
    codes = jnp.concatenate(lines, axis=0).astype(bf16)
    sub = lax.broadcasted_iota(jnp.int32, (4, 8, 128), 1)

    def binned(r):
        values = bin_index(feat_v[pl.ds(pl.multiple_of(r * 32, 32), 32), :])
        a = values[:, :128].reshape(4, 8, 128)
        b = values[:, 128:].reshape(4, 8, 128)
        first = jnp.where(sub < 4, a, pltpu.roll(b, 4, 1))
        second = jnp.where(sub < 4, pltpu.roll(a, 4, 1), b)
        return jnp.stack([first, second], axis=1).reshape(8, 8, 128).astype(bf16)

    def place(r, carry):
        send[r] = binned(r)
        return carry

    own_codes[...] = codes
    rbuf[0, 0, 1] = codes
    for q in range(CHUNKS):
        chunk_loads[q].wait()
        lax.fori_loop(q * (ROWS_AX // CHUNKS), (q + 1) * (ROWS_AX // CHUNKS), place, 0)
    rbuf[0, 0, 0] = send[my_rows, my_feat]
    acc[...] = jnp.zeros_like(acc)

    bins = (lax.broadcasted_iota(jnp.int32, (8, 16, 128), 0) * 16 + lax.broadcasted_iota(jnp.int32, (8, 16, 128), 1)).astype(f32).astype(bf16)
    classes = bins[: C // 16]

    def use(start, count):
        masks, targets = [], []
        for u in range(count):
            s = start + u
            for d in range(FEAT_AX):
                masks.append(mask_tile(rbuf[s, d, 0].astype(f32), bins))
                targets.append(target_tile(rbuf[s, d, 1].astype(f32), classes))
        acc[...] += lax.dot_general(jnp.concatenate(masks, axis=1), jnp.concatenate(targets, axis=1), NT, preferred_element_type=f32)

    others = pl.ds(1, FEAT_AX - 1)

    def push_features(s):
        def one(rows, feat, d):
            push(send.at[rows, feat], rbuf.at[s, d, 0], sent.at[0 if s == 0 else 1], feat_recv.at[s], rows, feat)

        to_column(s, one)

    def push_codes(s):
        def one(rows, feat, d):
            push(own_codes, rbuf.at[s, d, 1], sent.at[2 if s == 0 else 3], code_recv.at[s], rows, feat)

        to_column(s, one)

    pl.semaphore_wait(barrier, ROWS_AX * FEAT_AX - 1)
    for s in range(NEAR):
        push_codes(s)
        push_features(s)
        if s == 1:
            for far in range(NEAR, ROWS_AX):
                push(own_codes, rbuf.at[far, 0, 1], sent.at[4], far_recv.at[far], rows_peer(far), my_feat)
    for s in range(NEAR, ROWS_AX):
        push_features(s)

    wait_all(rbuf.at[0, others, 0], feat_recv.at[0])
    wait_all(rbuf.at[0, others, 1], code_recv.at[0])
    wait_all(rbuf.at[1, :, 0], feat_recv.at[1])
    wait_all(rbuf.at[1, :, 1], code_recv.at[1])
    use(0, 2)

    def pass_on(s, carry):
        wait_all(rbuf.at[s, 0, 1], far_recv.at[s])

        def one(d, inner):
            push(rbuf.at[s, 0, 1], rbuf.at[s, d, 1], sent.at[5], code_recv.at[s], my_rows, feat_peer(d))
            return inner

        lax.fori_loop(1, FEAT_AX, one, 0)
        return carry

    lax.fori_loop(NEAR, ROWS_AX, pass_on, 0)

    def step(g, carry):
        for u in range(2):
            s = 2 * g + u
            wait_all(rbuf.at[s, :, 0], feat_recv.at[s])

            @pl.when(g < NEAR // 2)
            def _():
                wait_all(rbuf.at[s, :, 1], code_recv.at[s])

            @pl.when(g >= NEAR // 2)
            def _():
                wait_all(rbuf.at[s, others, 1], code_recv.at[s])

        use(2 * g, 2)
        return carry

    lax.fori_loop(1, ROWS_AX // 2, step, 0)

    row_at = lax.broadcasted_iota(jnp.int32, (8, 128), 0)
    lane_at = lax.broadcasted_iota(jnp.int32, (8, 128), 1)
    gains = jnp.zeros((8, 128), f32)
    best = jnp.zeros((1, 128), f32)
    lane_row = lax.broadcasted_iota(jnp.int32, (1, 128), 1)
    for n in range(NODES):
        node_top = None
        for i in range(OWN):
            left = acc[i * B : (i + 1) * B, :].T[n * C : (n + 1) * C, :]
            total = left[:, B - 1 : B]
            right = total - left
            gain = ratio(left) + ratio(right) - ratio(total)
            top = jnp.max(gain, axis=1, keepdims=True)
            gains = jnp.where((row_at == n) & (lane_at == i), top, gains)
            node_top = top if node_top is None else jnp.maximum(node_top, top)
        best = jnp.where(lane_row == n, node_top, best)

    top_row[...] = best

    def push_top(s):
        def one(rows, feat, d):
            push(top_row, tops.at[s, d], sent.at[6 if s == 0 else 7], top_recv.at[0 if s == 0 else 1], rows, feat)

        to_column(s, one)

    for s in reversed(range(ROWS_AX)):
        push_top(s)
    rest, far_rest = pl.ds(1, ROWS_AX - 1), pl.ds(NEAR, ROWS_AX - NEAR)
    wait_all(rbuf.at[0, others, 0], sent.at[0])
    wait_all(rbuf.at[rest, :, 0], sent.at[1])
    wait_all(rbuf.at[0, others, 1], sent.at[2])
    wait_all(rbuf.at[pl.ds(1, NEAR - 1), :, 1], sent.at[3])
    wait_all(rbuf.at[far_rest, 0, 1], sent.at[4])
    wait_all(rbuf.at[far_rest, others, 1], sent.at[5])
    wait_all(tops.at[0, others], sent.at[6])
    wait_all(tops.at[rest], sent.at[7])
    wait_all(tops.at[0, others], top_recv.at[0])
    wait_all(tops.at[rest], top_recv.at[1])
    best = jnp.maximum(best, jnp.maximum(jnp.max(tops[0, 1:], axis=0), jnp.max(tops[1:], axis=(0, 1))))
    best_column = jnp.where(row_at == 0, best[:, 0:1], best[:, 1:2])
    out_ref[...] = jnp.where(lane_at < OWN, gains, best_column)


def local(features, labels, weights, nodes):
    dma = pltpu.SemaphoreType.DMA
    result = pl.pallas_call(
        kernel,
        out_shape=jax.ShapeDtypeStruct((8, 128), f32),
        in_specs=[pl.BlockSpec(memory_space=pl.ANY)] * 4,
        out_specs=pl.BlockSpec(memory_space=pltpu.VMEM),
        scratch_shapes=[
            pltpu.VMEM((512, LOCAL), f32),
            pltpu.VMEM((1, LOCAL), jnp.int32),
            pltpu.VMEM((1, LOCAL), bf16),
            pltpu.VMEM((1, LOCAL), jnp.int32),
            pltpu.VMEM((ROWS_AX, FEAT_AX, 8, 128), bf16),
            pltpu.VMEM((8, 128), bf16),
            pltpu.VMEM((ROWS_AX, FEAT_AX, 2, 8, 128), bf16),
            pltpu.VMEM((OWN * B, NODES * C), f32),
            pltpu.VMEM((1, 128), f32),
            pltpu.VMEM((ROWS_AX, FEAT_AX, 1, 128), f32),
            dma((CHUNKS + 3,)), dma((ROWS_AX,)), dma((ROWS_AX,)), dma((ROWS_AX,)), dma((2,)), dma((8,)),
        ],
        compiler_params=pltpu.CompilerParams(collective_id=0, has_side_effects=True, vmem_limit_bytes=48 * 1024 * 1024),
        name="split_scores",
    )(*[pltpu.with_memory_space_constraint(v, pltpu.HBM) for v in (features, labels.reshape(1, -1), weights, nodes)])
    return result[None, :NODES, :OWN], jnp.max(result[None, :NODES, OWN : 2 * OWN], axis=2)


def solution(mesh):
    return jax.shard_map(
        local,
        mesh=mesh,
        in_specs=(
            P(None, ("rows", "feat")),
            P(("rows", "feat")),
            P("leaf", ("rows", "feat")),
            P("leaf", ("rows", "feat")),
        ),
        out_specs=(P("leaf", None, ("rows", "feat")), P("leaf", None)),
        check_vma=False,
    )
```

time: 41.4 us -> 41.2 us (level)
  no operation moved by 1% of the time
where the time goes in v8:
time: 41.2 us; the launch traced here: 41.1 us
  Pallas kernels  39.3 us (95%)
  other arithmetic  1.19 us (3%)
  between operations  0.64 us (2%)
    pallas_call x1, Pallas kernels, local(): pl.pallas_call(kernel, out_shape=jax.ShapeDtypeStruct((8, 128), f32), in_...  39.3 us
    reduce_max x1, other arithmetic, local(): jnp.max(result[None, :NODES, OWN:2 * OWN], axis=2)  1.19 us

profile of v8, /device:TPU:1, one launch (start us, length us, event | category | flops | bytes accessed | tf_op | source)
XLA Modules:
  0.0 41.1 jit_solution(3267838886267845196)
XLA Ops:
  0.6 39.3 %split_scores.1 = f32[8,128]{1,0:T(8,128)S(1)} custom-call(f32[512,256]{1,0:T(8,128)} %feat_hbm.1, s32[1,256]{1,0:T(1,128)} %bitcast.4, bf16[1,256]{1,0:T(2,128)(2,1)} %wei_hbm.1, s32[1,256]{1,0:T(1,128)} %node_hbm.1), custom_call_target="tpu_custom_call" | custom-call | tf_op jit(solution)/shard_map/split_scores/pallas_call | solution.py:272
  39.9 1.2 %slice_reduce_fusion = (f32[2]{0:T(128)}, f32[1,2,4]{2,1,0:T(2,128)}) fusion(f32[8,128]{1,0:T(8,128)S(1)} %split_scores.1), kind=kLoop, calls=%fused_computation | loop fusion | flops 6 | bytes 104 | tf_op jit(solution)/shard_map/reduce_max | solution.py:293

commit v9 on v8

--- a/solution.py
+++ b/solution.py
@@ -83,11 +83,8 @@
     def to_column(s, action):
         rows = rows_peer(s)
 
-        def one(d, carry):
+        for d in range(1 if s == 0 else 0, FEAT_AX):
             action(rows, feat_peer(d), d)
-            return carry
-
-        lax.fori_loop(1 if s == 0 else 0, FEAT_AX, one, 0)
 
     def push(source, target, send_sem, recv_sem, rows, feat):
         pltpu.make_async_remote_copy(
@@ -197,11 +194,8 @@
     def pass_on(s, carry):
         wait_all(rbuf.at[s, 0, 1], far_recv.at[s])
 
-        def one(d, inner):
+        for d in range(1, FEAT_AX):
             push(rbuf.at[s, 0, 1], rbuf.at[s, d, 1], sent.at[5], code_recv.at[s], my_rows, feat_peer(d))
-            return inner
-
-        lax.fori_loop(1, FEAT_AX, one, 0)
         return carry
 
     lax.fori_loop(NEAR, ROWS_AX, pass_on, 0)

time: 41.2 us -> 41.9 us (1.017)
  Pallas kernels: 39.3 us -> 39.9 us
    pallas_call x1, Pallas kernels: 39.3 us -> 39.9 us  [local(): pl.pallas_call(kernel, out_shape=jax.ShapeDtypeStruct((8, 128), f32), in_...]
where the time goes in v9:
time: 41.9 us; the launch traced here: 41.8 us
  Pallas kernels  39.9 us (95%)
  other arithmetic  1.19 us (3%)
  between operations  0.64 us (2%)
    pallas_call x1, Pallas kernels, local(): pl.pallas_call(kernel, out_shape=jax.ShapeDtypeStruct((8, 128), f32), in_...  39.9 us
    reduce_max x1, other arithmetic, local(): jnp.max(result[None, :NODES, OWN:2 * OWN], axis=2)  1.19 us

profile of v9, /device:TPU:1, one launch (start us, length us, event | category | flops | bytes accessed | tf_op | source)
XLA Modules:
  0.0 41.8 jit_solution(8857257540147983161)
XLA Ops:
  0.6 39.9 %split_scores.1 = f32[8,128]{1,0:T(8,128)S(1)} custom-call(f32[512,256]{1,0:T(8,128)} %feat_hbm.1, s32[1,256]{1,0:T(1,128)} %bitcast.4, bf16[1,256]{1,0:T(2,128)(2,1)} %wei_hbm.1, s32[1,256]{1,0:T(1,128)} %node_hbm.1), custom_call_target="tpu_custom_call" | custom-call | tf_op jit(solution)/shard_map/split_scores/pallas_call | solution.py:266
  40.6 1.2 %slice_reduce_fusion = (f32[2]{0:T(128)}, f32[1,2,4]{2,1,0:T(2,128)}) fusion(f32[8,128]{1,0:T(8,128)S(1)} %split_scores.1), kind=kLoop, calls=%fused_computation | loop fusion | flops 6 | bytes 104 | tf_op jit(solution)/shard_map/reduce_max | solution.py:287

commit v10 on v8

--- a/solution.py
+++ b/solution.py
@@ -22,7 +22,6 @@
 MESH = pl.DeviceIdType.MESH
 NT = (((1,), (1,)), ((), ()))
 ORDER = [(0, 0), (0, 1), (1, 0), (7, 0), (1, 1), (7, 1), (2, 0), (6, 0), (2, 1), (6, 1), (3, 0), (5, 0), (3, 1), (5, 1), (4, 0), (4, 1)]
-NEAR = 6
 
 
 def bin_index(x):
@@ -67,8 +66,8 @@
 
 def kernel(
     feat_hbm, lab_hbm, wei_hbm, node_hbm, out_ref,
-    feat_v, lab_v, wei_v, node_v, send, own_codes, rbuf, acc, top_row, tops,
-    in_sem, feat_recv, code_recv, far_recv, top_recv, sent,
+    feat_v, lab_v, wei_v, node_v, send, rbuf, acc, top_row, tops,
+    in_sem, block_recv, top_recv, sent,
 ):
     my_rows, my_feat = lax.axis_index("rows"), lax.axis_index("feat")
     z, y = lax.div(my_rows, Y), lax.rem(my_rows, Y)
@@ -141,15 +140,14 @@
         return jnp.stack([first, second], axis=1).reshape(8, 8, 128).astype(bf16)
 
     def place(r, carry):
-        send[r] = binned(r)
+        send[r, :, 0] = binned(r)
+        send[r, :, 1] = jnp.broadcast_to(codes[None], (FEAT_AX, 8, 128))
         return carry
 
-    own_codes[...] = codes
-    rbuf[0, 0, 1] = codes
     for q in range(CHUNKS):
         chunk_loads[q].wait()
         lax.fori_loop(q * (ROWS_AX // CHUNKS), (q + 1) * (ROWS_AX // CHUNKS), place, 0)
-    rbuf[0, 0, 0] = send[my_rows, my_feat]
+    rbuf[0, 0] = send[my_rows, my_feat]
     acc[...] = jnp.zeros_like(acc)
 
     bins = (lax.broadcasted_iota(jnp.int32, (8, 16, 128), 0) * 16 + lax.broadcasted_iota(jnp.int32, (8, 16, 128), 1)).astype(f32).astype(bf16)
@@ -166,59 +164,23 @@
 
     others = pl.ds(1, FEAT_AX - 1)
 
-    def push_features(s):
+    def push_blocks(s):
         def one(rows, feat, d):
-            push(send.at[rows, feat], rbuf.at[s, d, 0], sent.at[0 if s == 0 else 1], feat_recv.at[s], rows, feat)
+            push(send.at[rows, feat], rbuf.at[s, d], sent.at[0 if s == 0 else 1], block_recv.at[s], rows, feat)
 
         to_column(s, one)
 
-    def push_codes(s):
-        def one(rows, feat, d):
-            push(own_codes, rbuf.at[s, d, 1], sent.at[2 if s == 0 else 3], code_recv.at[s], rows, feat)
-
-        to_column(s, one)
-
     pl.semaphore_wait(barrier, ROWS_AX * FEAT_AX - 1)
-    for s in range(NEAR):
-        push_codes(s)
-        push_features(s)
-        if s == 1:
-            for far in range(NEAR, ROWS_AX):
-                push(own_codes, rbuf.at[far, 0, 1], sent.at[4], far_recv.at[far], rows_peer(far), my_feat)
-    for s in range(NEAR, ROWS_AX):
-        push_features(s)
-
-    wait_all(rbuf.at[0, others, 0], feat_recv.at[0])
-    wait_all(rbuf.at[0, others, 1], code_recv.at[0])
-    wait_all(rbuf.at[1, :, 0], feat_recv.at[1])
-    wait_all(rbuf.at[1, :, 1], code_recv.at[1])
+    for s in range(ROWS_AX):
+        push_blocks(s)
+
+    wait_all(rbuf.at[0, others], block_recv.at[0])
+    wait_all(rbuf.at[1], block_recv.at[1])
     use(0, 2)
-
-    def pass_on(s, carry):
-        wait_all(rbuf.at[s, 0, 1], far_recv.at[s])
-
-        def one(d, inner):
-            push(rbuf.at[s, 0, 1], rbuf.at[s, d, 1], sent.at[5], code_recv.at[s], my_rows, feat_peer(d))
-            return inner
-
-        lax.fori_loop(1, FEAT_AX, one, 0)
-        return carry
-
-    lax.fori_loop(NEAR, ROWS_AX, pass_on, 0)
 
     def step(g, carry):
         for u in range(2):
-            s = 2 * g + u
-            wait_all(rbuf.at[s, :, 0], feat_recv.at[s])
-
-            @pl.when(g < NEAR // 2)
-            def _():
-                wait_all(rbuf.at[s, :, 1], code_recv.at[s])
-
-            @pl.when(g >= NEAR // 2)
-            def _():
-                wait_all(rbuf.at[s, others, 1], code_recv.at[s])
-
+            wait_all(rbuf.at[2 * g + u], block_recv.at[2 * g + u])
         use(2 * g, 2)
         return carry
 
@@ -245,21 +207,17 @@
 
     def push_top(s):
         def one(rows, feat, d):
-            push(top_row, tops.at[s, d], sent.at[6 if s == 0 else 7], top_recv.at[0 if s == 0 else 1], rows, feat)
+            push(top_row, tops.at[s, d], sent.at[2 if s == 0 else 3], top_recv.at[0 if s == 0 else 1], rows, feat)
 
         to_column(s, one)
 
     for s in reversed(range(ROWS_AX)):
         push_top(s)
-    rest, far_rest = pl.ds(1, ROWS_AX - 1), pl.ds(NEAR, ROWS_AX - NEAR)
-    wait_all(rbuf.at[0, others, 0], sent.at[0])
-    wait_all(rbuf.at[rest, :, 0], sent.at[1])
-    wait_all(rbuf.at[0, others, 1], sent.at[2])
-    wait_all(rbuf.at[pl.ds(1, NEAR - 1), :, 1], sent.at[3])
-    wait_all(rbuf.at[far_rest, 0, 1], sent.at[4])
-    wait_all(rbuf.at[far_rest, others, 1], sent.at[5])
-    wait_all(tops.at[0, others], sent.at[6])
-    wait_all(tops.at[rest], sent.at[7])
+    rest = pl.ds(1, ROWS_AX - 1)
+    wait_all(rbuf.at[0, others], sent.at[0])
+    wait_all(rbuf.at[rest], sent.at[1])
+    wait_all(tops.at[0, others], sent.at[2])
+    wait_all(tops.at[rest], sent.at[3])
     wait_all(tops.at[0, others], top_recv.at[0])
     wait_all(tops.at[rest], top_recv.at[1])
     best = jnp.maximum(best, jnp.maximum(jnp.max(tops[0, 1:], axis=0), jnp.max(tops[1:], axis=(0, 1))))
@@ -279,13 +237,12 @@
             pltpu.VMEM((1, LOCAL), jnp.int32),
             pltpu.VMEM((1, LOCAL), bf16),
             pltpu.VMEM((1, LOCAL), jnp.int32),
-            pltpu.VMEM((ROWS_AX, FEAT_AX, 8, 128), bf16),
-            pltpu.VMEM((8, 128), bf16),
+            pltpu.VMEM((ROWS_AX, FEAT_AX, 2, 8, 128), bf16),
             pltpu.VMEM((ROWS_AX, FEAT_AX, 2, 8, 128), bf16),
             pltpu.VMEM((OWN * B, NODES * C), f32),
             pltpu.VMEM((1, 128), f32),
             pltpu.VMEM((ROWS_AX, FEAT_AX, 1, 128), f32),
-            dma((CHUNKS + 3,)), dma((ROWS_AX,)), dma((ROWS_AX,)), dma((ROWS_AX,)), dma((2,)), dma((8,)),
+            dma((CHUNKS + 3,)), dma((ROWS_AX,)), dma((2,)), dma((4,)),
         ],
         compiler_params=pltpu.CompilerParams(collective_id=0, has_side_effects=True, vmem_limit_bytes=48 * 1024 * 1024),
         name="split_scores",

time: 41.2 us -> 44.3 us (1.075)
  Pallas kernels: 39.3 us -> 42.3 us
    pallas_call x1, Pallas kernels: 39.3 us -> 42.3 us  [local(): pl.pallas_call(kernel, out_shape=jax.ShapeDtypeStruct((8, 128), f32), in_...]
where the time goes in v10:
time: 44.3 us; the launch traced here: 44.2 us
  Pallas kernels  42.3 us (95%)
  other arithmetic  1.19 us (3%)
  between operations  0.64 us (1%)
    pallas_call x1, Pallas kernels, local(): pl.pallas_call(kernel, out_shape=jax.ShapeDtypeStruct((8, 128), f32), in_...  42.3 us
    reduce_max x1, other arithmetic, local(): jnp.max(result[None, :NODES, OWN:2 * OWN], axis=2)  1.19 us

profile of v10, /device:TPU:1, one launch (start us, length us, event | category | flops | bytes accessed | tf_op | source)
XLA Modules:
  0.0 44.2 jit_solution(4874919058315488111)
XLA Ops:
  0.6 42.3 %split_scores.1 = f32[8,128]{1,0:T(8,128)S(1)} custom-call(f32[512,256]{1,0:T(8,128)} %feat_hbm.1, s32[1,256]{1,0:T(1,128)} %bitcast.4, bf16[1,256]{1,0:T(2,128)(2,1)} %wei_hbm.1, s32[1,256]{1,0:T(1,128)} %node_hbm.1), custom_call_target="tpu_custom_call" | custom-call | tf_op jit(solution)/shard_map/split_scores/pallas_call | solution.py:230
  43.0 1.2 %slice_reduce_fusion = (f32[2]{0:T(128)}, f32[1,2,4]{2,1,0:T(2,128)}) fusion(f32[8,128]{1,0:T(8,128)S(1)} %split_scores.1), kind=kLoop, calls=%fused_computation | loop fusion | flops 6 | bytes 104 | tf_op jit(solution)/shard_map/reduce_max | solution.py:250

commit v11 on v7

--- a/solution.py
+++ b/solution.py
@@ -67,8 +67,8 @@
 
 def kernel(
     feat_hbm, lab_hbm, wei_hbm, node_hbm, out_ref,
-    feat_v, lab_v, wei_v, node_v, send, zbuf, rbuf, acc, m1s, m1, m2s, m2,
-    relay, in_sem, s1_send, s1_recv, s2_send, s2_recv, m1_send, m1_recv, m2_send, m2_recv,
+    feat_v, lab_v, wei_v, node_v, send, zbuf, rbuf, acc, top_row, tops,
+    relay, in_sem, s1_send, s1_recv, s2_send, s2_recv, near_send, near_recv, top_send, top_recv,
 ):
     my_rows, my_feat = lax.axis_index("rows"), lax.axis_index("feat")
     z, y = lax.div(my_rows, Y), lax.rem(my_rows, Y)
@@ -220,26 +220,27 @@
             node_top = top if node_top is None else jnp.maximum(node_top, top)
         best = jnp.where(lane_row == n, node_top, best)
 
-    m1s[...] = best
-    for d in range(1, FEAT_AX):
-        pltpu.make_async_remote_copy(
-            src_ref=m1s, dst_ref=m1.at[d], send_sem=m1_send, recv_sem=m1_recv,
-            device_id={"feat": feat_peer(d)}, device_id_type=MESH).start()
-    m1_all, m2_all = m1.at[pl.ds(1, FEAT_AX - 1)], m2.at[pl.ds(1, ROWS_AX - 1)]
-    pltpu.make_async_copy(m1_all, m1_all, m1_recv).wait()
-    best = jnp.maximum(best, jnp.max(m1[1:], axis=0))
-    m2s[...] = best
-    for s in range(1, ROWS_AX):
-        pltpu.make_async_remote_copy(
-            src_ref=m2s, dst_ref=m2.at[s], send_sem=m2_send, recv_sem=m2_recv,
-            device_id={"rows": rows_peer(*ORDER[s])}, device_id_type=MESH).start()
+    top_row[...] = best
+    for s in reversed(range(ROWS_AX)):
+        rows = rows_peer(*ORDER[s])
+
+        def push_top(d, carry, s=s, rows=rows):
+            pltpu.make_async_remote_copy(
+                src_ref=top_row, dst_ref=tops.at[s, d],
+                send_sem=near_send if s == 0 else top_send, recv_sem=near_recv if s == 0 else top_recv,
+                device_id={"rows": rows, "feat": feat_peer(d)}, device_id_type=MESH).start()
+            return carry
+
+        lax.fori_loop(1 if s == 0 else 0, FEAT_AX, push_top, 0)
     z_all, r_all = zbuf.at[pl.ds(1, ROWS_AX - 1)], rbuf.at[:, pl.ds(1, FEAT_AX - 1)]
     pltpu.make_async_copy(z_all, z_all, s1_send).wait()
     pltpu.make_async_copy(r_all, r_all, s2_send).wait()
-    pltpu.make_async_copy(m1_all, m1_all, m1_send).wait()
-    pltpu.make_async_copy(m2_all, m2_all, m2_send).wait()
-    pltpu.make_async_copy(m2_all, m2_all, m2_recv).wait()
-    best = jnp.maximum(best, jnp.max(m2[1:], axis=0))
+    near_tops, far_tops = tops.at[0, pl.ds(1, FEAT_AX - 1)], tops.at[pl.ds(1, ROWS_AX - 1)]
+    pltpu.make_async_copy(near_tops, near_tops, near_send).wait()
+    pltpu.make_async_copy(far_tops, far_tops, top_send).wait()
+    pltpu.make_async_copy(near_tops, near_tops, near_recv).wait()
+    pltpu.make_async_copy(far_tops, far_tops, top_recv).wait()
+    best = jnp.maximum(best, jnp.maximum(jnp.max(tops[0, 1:], axis=0), jnp.max(tops[1:], axis=(0, 1))))
     best_column = jnp.where(row_at == 0, best[:, 0:1], best[:, 1:2])
     out_ref[...] = jnp.where(lane_at < OWN, gains, best_column)
 
@@ -261,9 +262,7 @@
             pltpu.VMEM((ROWS_AX, FEAT_AX, 2, 8, 128), bf16),
             pltpu.VMEM((OWN * B, NODES * C), f32),
             pltpu.VMEM((1, 128), f32),
-            pltpu.VMEM((FEAT_AX, 1, 128), f32),
-            pltpu.VMEM((1, 128), f32),
-            pltpu.VMEM((ROWS_AX, 1, 128), f32),
+            pltpu.VMEM((ROWS_AX, FEAT_AX, 1, 128), f32),
             pltpu.SemaphoreType.REGULAR((len(LEVELS) - 1, 2)),
             dma((CHUNKS + 3,)), dma(()), dma((ROWS_AX,)), dma(()), dma((ROWS_AX,)), dma(()), dma(()), dma(()), dma(()),
         ],

time: 41.4 us -> 41.4 us (level)
  no operation moved by 1% of the time
where the time goes in v11:
time: 41.4 us; the launch traced here: 41.3 us
  Pallas kernels  39.4 us (95%)
  other arithmetic  1.19 us (3%)
  between operations  0.64 us (2%)
    pallas_call x1, Pallas kernels, local(): pl.pallas_call(kernel, out_shape=jax.ShapeDtypeStruct((8, 128), f32), in_...  39.4 us
    reduce_max x1, other arithmetic, local(): jnp.max(result[None, :NODES, OWN:2 * OWN], axis=2)  1.19 us

profile of v11, /device:TPU:1, one launch (start us, length us, event | category | flops | bytes accessed | tf_op | source)
XLA Modules:
  0.0 41.3 jit_solution(6703371313362400985)
XLA Ops:
  0.6 39.4 %split_scores.1 = f32[8,128]{1,0:T(8,128)S(1)} custom-call(f32[512,256]{1,0:T(8,128)} %feat_hbm.1, s32[1,256]{1,0:T(1,128)} %bitcast.4, bf16[1,256]{1,0:T(2,128)(2,1)} %wei_hbm.1, s32[1,256]{1,0:T(1,128)} %node_hbm.1), custom_call_target="tpu_custom_call" | custom-call | tf_op jit(solution)/shard_map/split_scores/pallas_call | solution.py:250
  40.1 1.2 %slice_reduce_fusion = (f32[2]{0:T(128)}, f32[1,2,4]{2,1,0:T(2,128)}) fusion(f32[8,128]{1,0:T(8,128)S(1)} %split_scores.1), kind=kLoop, calls=%fused_computation | loop fusion | flops 6 | bytes 104 | tf_op jit(solution)/shard_map/reduce_max | solution.py:272

commit v12 on v8

--- a/solution.py
+++ b/solution.py
@@ -241,16 +241,18 @@
             node_top = top if node_top is None else jnp.maximum(node_top, top)
         best = jnp.where(lane_row == n, node_top, best)
 
-    top_row[...] = best
-
-    def push_top(s):
-        def one(rows, feat, d):
-            push(top_row, tops.at[s, d], sent.at[6 if s == 0 else 7], top_recv.at[0 if s == 0 else 1], rows, feat)
-
-        to_column(s, one)
-
-    for s in reversed(range(ROWS_AX)):
-        push_top(s)
+    top_row[0] = best
+
+    def push_near(d, carry):
+        push(top_row.at[0], tops.at[0, d], sent.at[6], top_recv.at[0], my_rows, feat_peer(d))
+        return carry
+
+    lax.fori_loop(1, FEAT_AX, push_near, 0)
+    wait_all(tops.at[0, others], top_recv.at[0])
+    best = jnp.maximum(best, jnp.max(tops[0, 1:], axis=0))
+    top_row[1] = best
+    for s in reversed(range(1, ROWS_AX)):
+        push(top_row.at[1], tops.at[s, 0], sent.at[7], top_recv.at[1], rows_peer(s), my_feat)
     rest, far_rest = pl.ds(1, ROWS_AX - 1), pl.ds(NEAR, ROWS_AX - NEAR)
     wait_all(rbuf.at[0, others, 0], sent.at[0])
     wait_all(rbuf.at[rest, :, 0], sent.at[1])
@@ -259,10 +261,9 @@
     wait_all(rbuf.at[far_rest, 0, 1], sent.at[4])
     wait_all(rbuf.at[far_rest, others, 1], sent.at[5])
     wait_all(tops.at[0, others], sent.at[6])
-    wait_all(tops.at[rest], sent.at[7])
-    wait_all(tops.at[0, others], top_recv.at[0])
-    wait_all(tops.at[rest], top_recv.at[1])
-    best = jnp.maximum(best, jnp.maximum(jnp.max(tops[0, 1:], axis=0), jnp.max(tops[1:], axis=(0, 1))))
+    wait_all(tops.at[rest, 0], sent.at[7])
+    wait_all(tops.at[rest, 0], top_recv.at[1])
+    best = jnp.maximum(best, jnp.max(tops[1:, 0], axis=0))
     best_column = jnp.where(row_at == 0, best[:, 0:1], best[:, 1:2])
     out_ref[...] = jnp.where(lane_at < OWN, gains, best_column)
 
@@ -283,7 +284,7 @@
             pltpu.VMEM((8, 128), bf16),
             pltpu.VMEM((ROWS_AX, FEAT_AX, 2, 8, 128), bf16),
             pltpu.VMEM((OWN * B, NODES * C), f32),
-            pltpu.VMEM((1, 128), f32),
+            pltpu.VMEM((2, 1, 128), f32),
             pltpu.VMEM((ROWS_AX, FEAT_AX, 1, 128), f32),
             dma((CHUNKS + 3,)), dma((ROWS_AX,)), dma((ROWS_AX,)), dma((ROWS_AX,)), dma((2,)), dma((8,)),
         ],

time: 41.2 us -> 41.6 us (level)
  no operation moved by 1% of the time
where the time goes in v12:
time: 41.6 us; the launch traced here: 41.4 us
  Pallas kernels  39.6 us (95%)
  other arithmetic  1.19 us (3%)
  between operations  0.64 us (2%)
    pallas_call x1, Pallas kernels, local(): pl.pallas_call(kernel, out_shape=jax.ShapeDtypeStruct((8, 128), f32), in_...  39.6 us
    reduce_max x1, other arithmetic, local(): jnp.max(result[None, :NODES, OWN:2 * OWN], axis=2)  1.19 us

profile of v12, /device:TPU:1, one launch (start us, length us, event | category | flops | bytes accessed | tf_op | source)
XLA Modules:
  0.0 41.4 jit_solution(15882817539416877166)
XLA Ops:
  0.6 39.6 %split_scores.1 = f32[8,128]{1,0:T(8,128)S(1)} custom-call(f32[512,256]{1,0:T(8,128)} %feat_hbm.1, s32[1,256]{1,0:T(1,128)} %bitcast.4, bf16[1,256]{1,0:T(2,128)(2,1)} %wei_hbm.1, s32[1,256]{1,0:T(1,128)} %node_hbm.1), custom_call_target="tpu_custom_call" | custom-call | tf_op jit(solution)/shard_map/split_scores/pallas_call | solution.py:273
  40.2 1.2 %slice_reduce_fusion = (f32[2]{0:T(128)}, f32[1,2,4]{2,1,0:T(2,128)}) fusion(f32[8,128]{1,0:T(8,128)S(1)} %split_scores.1), kind=kLoop, calls=%fused_computation | loop fusion | flops 6 | bytes 104 | tf_op jit(solution)/shard_map/reduce_max | solution.py:294
